TPU v7x, 256 devices: a whole 4x4x8 slice. The times are simulated.
256 devices in a mesh: clip: 16 (over z_hi, x), frame: 16 (over y, z_lo, core).
Axes of the slice: x: 4, y: 4, z: 8 (z_hi: 4, z_lo: 2; z = z_hi * 2 + z_lo), core: 2. Of those that a mesh axis runs over, the one named last changes fastest.
Arguments:
- frames_in: bfloat16 [16, 32, 96, 1280], P('clip', 'frame'), may hold values from -6 to 6
- ref_feats: bfloat16 [16, 96, 1280], P('clip', 'frame'), may hold values from -6 to 6
- out_grad: bfloat16 [16, 32, 96, 1280], P('clip', 'frame'), may hold values from -6 to 6
- space_query: bfloat16 [1280, 640], P('frame'), may hold values from -0.15625 to 0.15625
- space_key: bfloat16 [1280, 640], P('frame'), may hold values from -0.15625 to 0.15625
- space_value: bfloat16 [1280, 640], P('frame'), may hold values from -0.15625 to 0.15625
- space_output: bfloat16 [640, 1280], P('frame'), may hold values from -0.25 to 0.25
- time_query: bfloat16 [1280, 640], P('frame'), may hold values from -0.15625 to 0.15625
- time_key: bfloat16 [1280, 640], P('frame'), may hold values from -0.15625 to 0.15625
- time_value: bfloat16 [1280, 640], P('frame'), may hold values from -0.15625 to 0.15625
- time_output: bfloat16 [640, 1280], P('frame'), may hold values from -0.25 to 0.25
Outputs:
- out: bfloat16 [16, 32, 96, 1280], P('clip', 'frame')
- frames_grad: bfloat16 [16, 32, 96, 1280], P('clip', 'frame')
- ref_grad: bfloat16 [16, 96, 1280], P('clip', 'frame')
- space_query_grad: float32 [1280, 640], P('frame')
- space_key_grad: float32 [1280, 640], P('frame')
- space_value_grad: float32 [1280, 640], P('frame')
- space_output_grad: float32 [640, 1280], P('frame')
- time_query_grad: float32 [1280, 640], P('frame')
- time_key_grad: float32 [1280, 640], P('frame')
- time_value_grad: float32 [1280, 640], P('frame')
- time_output_grad: float32 [640, 1280], P('frame')
All inputs are finite; a program needn't handle non-finite values.
Results may differ from a plain program's by a relative error of at most 0.035.
Values may be sent and summed in bfloat16 or wider, within the bound.
A program may use at most 128 MiB of HBM per device.

v0:
```python
import math

import jax
import jax.numpy as jnp
from jax import lax
from jax.sharding import PartitionSpec as P

HEADS = 4


EPSILON = 1e-05


def layer_stats(rows):
    wide = rows.astype(jnp.float32)
    centre = jnp.mean(wide, -1, keepdims=True)
    offset = wide - centre
    inverse = lax.rsqrt(jnp.mean(offset * offset, -1, keepdims=True) + EPSILON)
    return (offset * inverse, inverse)


def layer_back(centred, inverse, cotangent):
    first = jnp.mean(cotangent, -1, keepdims=True)
    second = jnp.mean(cotangent * centred, -1, keepdims=True)
    return inverse * (cotangent - first - centred * second)


def position_table(first, count, width):
    frame_ids = (first + jnp.arange(count, dtype=jnp.int32)).astype(jnp.float32)
    halves = jnp.arange(width // 2, dtype=jnp.int32).astype(jnp.float32)
    rates = jnp.exp(halves * (-2.0 * math.log(10000.0) / width))
    angles = frame_ids[:, None] * rates[None, :]
    return jnp.stack([jnp.sin(angles), jnp.cos(angles)], -1).reshape(count, width)


def einsum_forms(temporal):
    if temporal:
        return ("qbhe,kbhe->bhqk", "bhqk,kbhe->qbhe", "bhqk,qbhe->kbhe")
    return ("bqhe,bkhe->bhqk", "bhqk,bkhe->bqhe", "bhqk,bqhe->bkhe")


def product(form, left, right):
    return jnp.einsum(form, left, right, preferred_element_type=jnp.float32)


def attention(query, keys, values, temporal):
    score_form, mix_form, back_form = einsum_forms(temporal)
    scores = product(score_form, query, keys) * query.shape[-1] ** (-0.5)
    powers = jnp.exp(scores)
    probs = powers / jnp.sum(powers, -1, keepdims=True)
    rounded = probs.astype(jnp.bfloat16)
    mixed = product(mix_form, rounded, values).astype(jnp.bfloat16)
    return (mixed, probs, rounded)


def attention_back(query, keys, values, probs, rounded, cotangent, temporal):
    score_form, mix_form, back_form = einsum_forms(temporal)
    prob_grad = product(score_form, cotangent, values)
    score_grad = probs * (prob_grad - jnp.sum(probs * prob_grad, -1, keepdims=True))
    score_rounded = (score_grad * query.shape[-1] ** (-0.5)).astype(jnp.bfloat16)
    query_grad = product(mix_form, score_rounded, keys).astype(jnp.bfloat16)
    key_grad = product(back_form, score_rounded, query)
    value_grad = product(back_form, rounded, cotangent)
    return (query_grad, key_grad, value_grad)


def split_heads(rows):
    return rows.reshape(rows.shape[:-1] + (HEADS, rows.shape[-1] // HEADS))


def merge_heads(rows):
    return rows.reshape(rows.shape[:-2] + (rows.shape[-2] * rows.shape[-1],))


def project(rows, weight):
    flat_rows = rows.reshape(-1, rows.shape[-1])
    result = jnp.dot(flat_rows, weight, preferred_element_type=jnp.float32)
    return result.reshape(rows.shape[:-1] + (weight.shape[1],))


def project_back(rows, weight):
    flat_rows = rows.reshape(-1, rows.shape[-1])
    result = lax.dot_general(
        flat_rows, weight, (((1,), (1,)), ((), ())), preferred_element_type=jnp.float32
    )
    return result.reshape(rows.shape[:-1] + (weight.shape[0],))


def outer_sum(left, right):
    left_rows = left.reshape(-1, left.shape[-1])
    right_rows = right.reshape(-1, right.shape[-1])
    return lax.dot_general(
        left_rows, right_rows, (((0,), (0,)), ((), ())), preferred_element_type=jnp.float32
    )


def per_device(
    frames_in,
    ref_feats,
    out_grad,
    space_query,
    space_key,
    space_value,
    space_output,
    time_query,
    time_key,
    time_value,
    time_output,
):
    block = lax.axis_index("frame")
    (
        full_space_query,
        full_space_key,
        full_space_value,
        full_space_output,
        full_time_query,
        full_time_key,
        full_time_value,
        full_time_output,
    ) = (
        lax.all_gather(space_query, "frame", axis=0, tiled=True),
        lax.all_gather(space_key, "frame", axis=0, tiled=True),
        lax.all_gather(space_value, "frame", axis=0, tiled=True),
        lax.all_gather(space_output, "frame", axis=0, tiled=True),
        lax.all_gather(time_query, "frame", axis=0, tiled=True),
        lax.all_gather(time_key, "frame", axis=0, tiled=True),
        lax.all_gather(time_value, "frame", axis=0, tiled=True),
        lax.all_gather(time_output, "frame", axis=0, tiled=True),
    )
    frames = frames_in[0]
    refer = ref_feats[0]
    cotangent = out_grad[0]
    frame_count = frames.shape[0]
    token_count = frames.shape[1]
    centred_one, inverse_one = layer_stats(frames)
    normed_one = centred_one.astype(jnp.bfloat16)
    spatial_query = project(normed_one, full_space_query).astype(jnp.bfloat16)
    spatial_key = project(normed_one, full_space_key).astype(jnp.bfloat16)
    spatial_value = project(normed_one, full_space_value).astype(jnp.bfloat16)
    own_key = project(refer, full_space_key).astype(jnp.bfloat16)
    own_value = project(refer, full_space_value).astype(jnp.bfloat16)
    refer_key, refer_value = (
        lax.all_gather(own_key, "frame", axis=0, tiled=True),
        lax.all_gather(own_value, "frame", axis=0, tiled=True),
    )
    keys_joined = jnp.concatenate(
        [spatial_key, jnp.broadcast_to(refer_key[None], spatial_key.shape)], 1
    )
    values_joined = jnp.concatenate(
        [spatial_value, jnp.broadcast_to(refer_value[None], spatial_value.shape)], 1
    )
    spatial_mixed, spatial_probs, spatial_rounded = attention(
        split_heads(spatial_query), split_heads(keys_joined), split_heads(values_joined), False
    )
    spatial_mixed = merge_heads(spatial_mixed)
    hidden_one = (frames.astype(jnp.float32) + project(spatial_mixed, full_space_output)).astype(
        jnp.bfloat16
    )
    centred_two, inverse_two = layer_stats(hidden_one)
    table = position_table(block * frame_count, frame_count, frames.shape[2])
    normed_two = (centred_two + table[:, None, :]).astype(jnp.bfloat16)
    local_query = project(normed_two, full_time_query).astype(jnp.bfloat16)
    local_key = project(normed_two, full_time_key).astype(jnp.bfloat16)
    local_value = project(normed_two, full_time_value).astype(jnp.bfloat16)
    temporal_query, temporal_key, temporal_value = (
        lax.all_to_all(local_query, "frame", split_axis=1, concat_axis=0, tiled=True),
        lax.all_to_all(local_key, "frame", split_axis=1, concat_axis=0, tiled=True),
        lax.all_to_all(local_value, "frame", split_axis=1, concat_axis=0, tiled=True),
    )
    temporal_mixed, temporal_probs, temporal_rounded = attention(
        split_heads(temporal_query), split_heads(temporal_key), split_heads(temporal_value), True
    )
    mixed_two = lax.all_to_all(
        merge_heads(temporal_mixed), "frame", split_axis=0, concat_axis=1, tiled=True
    )
    output = (hidden_one.astype(jnp.float32) + project(mixed_two, full_time_output)).astype(
        jnp.bfloat16
    )
    mixed_grad_two = project_back(cotangent, full_time_output).astype(jnp.bfloat16)
    token_grad = lax.all_to_all(mixed_grad_two, "frame", split_axis=1, concat_axis=0, tiled=True)
    token_query_grad, token_key_grad, token_value_grad = attention_back(
        split_heads(temporal_query),
        split_heads(temporal_key),
        split_heads(temporal_value),
        temporal_probs,
        temporal_rounded,
        split_heads(token_grad),
        True,
    )
    query_grad_two, key_grad_two, value_grad_two = (
        lax.all_to_all(
            merge_heads(token_query_grad), "frame", split_axis=0, concat_axis=1, tiled=True
        ),
        lax.all_to_all(
            merge_heads(token_key_grad).astype(jnp.bfloat16),
            "frame",
            split_axis=0,
            concat_axis=1,
            tiled=True,
        ),
        lax.all_to_all(
            merge_heads(token_value_grad).astype(jnp.bfloat16),
            "frame",
            split_axis=0,
            concat_axis=1,
            tiled=True,
        ),
    )
    normed_grad_two = (
        project_back(query_grad_two, full_time_query)
        + project_back(key_grad_two, full_time_key)
        + project_back(value_grad_two, full_time_value)
    )
    hidden_grad = (
        cotangent.astype(jnp.float32) + layer_back(centred_two, inverse_two, normed_grad_two)
    ).astype(jnp.bfloat16)
    mixed_grad_one = project_back(hidden_grad, full_space_output).astype(jnp.bfloat16)
    query_grad_one, key_joined_grad, value_joined_grad = attention_back(
        split_heads(spatial_query),
        split_heads(keys_joined),
        split_heads(values_joined),
        spatial_probs,
        spatial_rounded,
        split_heads(mixed_grad_one),
        False,
    )
    query_grad_one = merge_heads(query_grad_one)
    key_grad_one = merge_heads(key_joined_grad[:, :token_count]).astype(jnp.bfloat16)
    value_grad_one = merge_heads(value_joined_grad[:, :token_count]).astype(jnp.bfloat16)
    partial_key = merge_heads(jnp.sum(key_joined_grad[:, token_count:], 0))
    partial_value = merge_heads(jnp.sum(value_joined_grad[:, token_count:], 0))
    summed_key, summed_value = (
        lax.psum_scatter(
            partial_key.astype(jnp.bfloat16), "frame", scatter_dimension=0, tiled=True
        ).astype(jnp.float32),
        lax.psum_scatter(
            partial_value.astype(jnp.bfloat16), "frame", scatter_dimension=0, tiled=True
        ).astype(jnp.float32),
    )
    refer_key_grad = summed_key.astype(jnp.bfloat16)
    refer_value_grad = summed_value.astype(jnp.bfloat16)
    normed_grad_one = (
        project_back(query_grad_one, full_space_query)
        + project_back(key_grad_one, full_space_key)
        + project_back(value_grad_one, full_space_value)
    )
    frames_grad = (
        hidden_grad.astype(jnp.float32) + layer_back(centred_one, inverse_one, normed_grad_one)
    ).astype(jnp.bfloat16)
    refer_grad = (
        project_back(refer_key_grad, full_space_key)
        + project_back(refer_value_grad, full_space_value)
    ).astype(jnp.bfloat16)
    term_sq = outer_sum(normed_one, query_grad_one)
    term_sk = outer_sum(normed_one, key_grad_one) + outer_sum(refer, refer_key_grad)
    term_sv = outer_sum(normed_one, value_grad_one) + outer_sum(refer, refer_value_grad)
    term_so = outer_sum(spatial_mixed, hidden_grad)
    term_tq = outer_sum(normed_two, query_grad_two)
    term_tk = outer_sum(normed_two, key_grad_two)
    term_tv = outer_sum(normed_two, value_grad_two)
    term_to = outer_sum(mixed_two, cotangent)
    share_sq, share_sk, share_sv, share_so, share_tq, share_tk, share_tv, share_to = (
        lax.psum_scatter(
            term_sq.astype(jnp.bfloat16), "frame", scatter_dimension=0, tiled=True
        ).astype(jnp.float32),
        lax.psum_scatter(
            term_sk.astype(jnp.bfloat16), "frame", scatter_dimension=0, tiled=True
        ).astype(jnp.float32),
        lax.psum_scatter(
            term_sv.astype(jnp.bfloat16), "frame", scatter_dimension=0, tiled=True
        ).astype(jnp.float32),
        lax.psum_scatter(
            term_so.astype(jnp.bfloat16), "frame", scatter_dimension=0, tiled=True
        ).astype(jnp.float32),
        lax.psum_scatter(
            term_tq.astype(jnp.bfloat16), "frame", scatter_dimension=0, tiled=True
        ).astype(jnp.float32),
        lax.psum_scatter(
            term_tk.astype(jnp.bfloat16), "frame", scatter_dimension=0, tiled=True
        ).astype(jnp.float32),
        lax.psum_scatter(
            term_tv.astype(jnp.bfloat16), "frame", scatter_dimension=0, tiled=True
        ).astype(jnp.float32),
        lax.psum_scatter(
            term_to.astype(jnp.bfloat16), "frame", scatter_dimension=0, tiled=True
        ).astype(jnp.float32),
    )
    total_sq, total_sk, total_sv, total_so, total_tq, total_tk, total_tv, total_to = (
        lax.psum(share_sq.astype(jnp.bfloat16), "clip").astype(jnp.float32),
        lax.psum(share_sk.astype(jnp.bfloat16), "clip").astype(jnp.float32),
        lax.psum(share_sv.astype(jnp.bfloat16), "clip").astype(jnp.float32),
        lax.psum(share_so.astype(jnp.bfloat16), "clip").astype(jnp.float32),
        lax.psum(share_tq.astype(jnp.bfloat16), "clip").astype(jnp.float32),
        lax.psum(share_tk.astype(jnp.bfloat16), "clip").astype(jnp.float32),
        lax.psum(share_tv.astype(jnp.bfloat16), "clip").astype(jnp.float32),
        lax.psum(share_to.astype(jnp.bfloat16), "clip").astype(jnp.float32),
    )
    return (
        output[None],
        frames_grad[None],
        refer_grad[None],
        total_sq,
        total_sk,
        total_sv,
        total_so,
        total_tq,
        total_tk,
        total_tv,
        total_to,
    )


def solution(mesh):
    in_specs = (
        P("clip", "frame", None, None),
        P("clip", "frame", None),
        P("clip", "frame", None, None),
        P("frame", None),
        P("frame", None),
        P("frame", None),
        P("frame", None),
        P("frame", None),
        P("frame", None),
        P("frame", None),
        P("frame", None),
    )
    out_specs = (
        P("clip", "frame", None, None),
        P("clip", "frame", None, None),
        P("clip", "frame", None),
        P("frame", None),
        P("frame", None),
        P("frame", None),
        P("frame", None),
        P("frame", None),
        P("frame", None),
        P("frame", None),
        P("frame", None),
    )
    return jax.shard_map(
        per_device, mesh=mesh, in_specs=in_specs, out_specs=out_specs, check_vma=False
    )
```

profile of v0, /device:TPU:32, one launch (start us, length us, event | category | flops | bytes accessed | tf_op | source)
XLA Modules:
  0.0 1246.3 jit_solution(11171798281253957471)
XLA Ops:
  15.1 32.6 %all-gather.15.cloned.1.call-done = bf16[1280,640]{1,0:T(8,128)(2,1)} async-done(((bf16[80,640]{1,0:T(8,128)(2,1)}), bf16[1280,640]{1,0:T(8,128)(2,1)}) %all-gather.15.cloned.1.call-update) | async-done | bytes 1638416 | tf_op jit(solution)/shard_map/all_gather | solution.py:122
  49.6 17.3 %all-gather.1 = bf16[16,6,640]{2,1,0:T(8,128)(2,1)S(1)} all-gather(bf16[1,6,640]{2,1,0:T(8,128)(2,1)S(1)} %fusion.83), channel_id=1, replica_groups=mesh['clip'=16,'frame'=16] {'frame'}, dimensions={0}, use_global_device_ids=true | all-gather | bytes 130560 | tf_op jit(solution)/shard_map/all_gather | solution.py:143
  67.9 17.4 %all-gather.13.cloned.1.call-done = bf16[1280,640]{1,0:T(8,128)(2,1)} async-done(((bf16[80,640]{1,0:T(8,128)(2,1)}), bf16[1280,640]{1,0:T(8,128)(2,1)}) %all-gather.13.cloned.1.call-update) | async-done | bytes 1638416 | tf_op jit(solution)/shard_map/all_gather | solution.py:121
  85.3 2.0 fusion.55
  87.6 35.2 %all-gather.11.cloned.1.call-done = bf16[1280,640]{1,0:T(8,128)(2,1)} async-done(((bf16[80,640]{1,0:T(8,128)(2,1)}), bf16[1280,640]{1,0:T(8,128)(2,1)}) %all-gather.11.cloned.1.call-update) | async-done | bytes 1638416 | tf_op jit(solution)/shard_map/all_gather | solution.py:123
  124.6 17.2 %all-gather = bf16[16,6,640]{2,1,0:T(8,128)(2,1)S(1)} all-gather(bf16[1,6,640]{2,1,0:T(8,128)(2,1)S(1)} %fusion.82), channel_id=1, replica_groups=mesh['clip'=16,'frame'=16] {'frame'}, dimensions={0}, use_global_device_ids=true | all-gather | bytes 130560 | tf_op jit(solution)/shard_map/all_gather | solution.py:144
  144.1 2.0 convolution_convert_fusion.11
  146.2 13.9 %all-gather.17.cloned.1.call-done = bf16[640,1280]{1,0:T(8,128)(2,1)} async-done(((bf16[40,1280]{1,0:T(8,128)(2,1)}), bf16[640,1280]{1,0:T(8,128)(2,1)}) %all-gather.17.cloned.1.call-update) | async-done | bytes 1638416 | tf_op jit(solution)/shard_map/all_gather | solution.py:124
  160.1 2.1 fusion.159
  162.7 34.8 %all-gather.21.cloned.1.call-done = bf16[1280,640]{1,0:T(8,128)(2,1)} async-done(((bf16[80,640]{1,0:T(8,128)(2,1)}), bf16[1280,640]{1,0:T(8,128)(2,1)}) %all-gather.21.cloned.1.call-update) | async-done | bytes 1638416 | tf_op jit(solution)/shard_map/all_gather | solution.py:125
  197.5 2.0 fusion.67
  200.4 4.8 all-to-all-start.1
  205.2 29.7 %all-gather.23.cloned.1.call-done = bf16[1280,640]{1,0:T(8,128)(2,1)} async-done(((bf16[80,640]{1,0:T(8,128)(2,1)}), bf16[1280,640]{1,0:T(8,128)(2,1)}) %all-gather.23.cloned.1.call-update) | async-done | bytes 1638416 | tf_op jit(solution)/shard_map/all_gather | solution.py:126
  234.9 2.0 fusion.70
  237.8 4.8 all-to-all-start.2
  242.6 29.8 %all-gather.19.cloned.1.call-done = bf16[1280,640]{1,0:T(8,128)(2,1)} async-done(((bf16[80,640]{1,0:T(8,128)(2,1)}), bf16[1280,640]{1,0:T(8,128)(2,1)}) %all-gather.19.cloned.1.call-update) | async-done | bytes 1638416 | tf_op jit(solution)/shard_map/all_gather | solution.py:127
  272.5 2.0 fusion.64
  275.4 4.8 all-to-all-start
  280.2 29.8 %all-gather.25.cloned.1.call-done = bf16[640,1280]{1,0:T(8,128)(2,1)} async-done(((bf16[40,1280]{1,0:T(8,128)(2,1)}), bf16[640,1280]{1,0:T(8,128)(2,1)}) %all-gather.25.cloned.1.call-update) | async-done | bytes 1638416 | tf_op jit(solution)/shard_map/all_gather | solution.py:128
  310.0 2.1 fusion.73
  313.9 2.1 reshape.372
  317.3 5.4 all-to-all-start.4
  330.8 2.1 reshape.375
  332.8 2.0 fusion.109
  334.8 2.5 fusion.46
  339.7 5.7 all-to-all-start.6
  345.4 2.6 fusion.45
  348.0 2.0 copy.158
  350.1 2.1 reshape.399
  353.7 5.0 all-to-all-start.5
  358.6 2.2 fusion.47
  360.9 2.0 copy.164
  362.9 2.1 reshape.401
  366.9 4.6 all-to-all-start.7
  371.6 2.0 copy.140
  373.5 2.0 reshape_reshape.9
  375.5 2.5 fusion.105
  380.0 2.4 fusion.18
  389.5 3.0 convolution_bitcast_fusion.4
  392.4 2.5 fusion.160
  395.9 3.4 convolution_bitcast_fusion.5
  399.2 2.3 slice_reduce_fusion.1
  401.6 2.8 convolution_convert_fusion.4
  405.0 2.0 convolution_convert_fusion.2
  407.4 3.2 convolution_convert_fusion.10
  412.7 2.9 convolution_convert_fusion.5
  416.1 1.9 convolution_convert_fusion.3
  419.2 2.9 convolution_convert_fusion.1
  422.2 2.2 fusion.44
  426.0 13.1 %all_to_all.120 = bf16[32,6,640]{2,1,0:T(8,128)(2,1)S(1)} all-to-all(bf16[32,6,640]{2,1,0:T(8,128)(2,1)S(1)} %reshape.398), channel_id=1, replica_groups=mesh['clip'=16,'frame'=16] {'frame'}, dimensions={0} | all-to-all | bytes 491520 | tf_op jit(solution)/shard_map/all_to_all | solution.py:173
  444.5 2.4 convolution_bitcast_fusion.1
  446.9 74.2 %all-reduce.7.cloned.1.call-done = (bf16[96,640]{0,1:T(8,128)(2,1)}, bf16[96,640]{0,1:T(8,128)(2,1)}) async-done(((bf16[96,640]{0,1:T(8,128)(2,1)}, bf16[96,640]{0,1:T(8,128)(2,1)}), (bf16[96,640]{0,1:T(8,128)(2,1)}, bf16[96,640]{0,1:T(8,128)(2,1)})) %all-reduce.7.cloned.1.call-update) | async-done | bytes 245776
  521.1 3.9 fusion.5
  527.3 1.9 fusion.4
  535.5 51.4 %reduce-scatter.17.cloned.1.call-done = bf16[40,1280]{1,0:T(8,128)(2,1)} async-done(((bf16[640,1280]{1,0:T(8,128)(2,1)}), bf16[40,1280]{1,0:T(8,128)(2,1)}) %reduce-scatter.17.cloned.1.call-update) | async-done | bytes 102416 | tf_op jit(solution)/shard_map/reduce_scatter | solution.py:272
  586.8 66.9 %reduce-scatter.21.cloned.1.call-done = bf16[80,640]{1,0:T(8,128)(2,1)} async-done(((bf16[1280,640]{1,0:T(8,128)(2,1)}), bf16[80,640]{1,0:T(8,128)(2,1)}) %reduce-scatter.21.cloned.1.call-update) | async-done | bytes 102416 | tf_op jit(solution)/shard_map/reduce_scatter | solution.py:278
  653.7 66.7 %reduce-scatter.11.cloned.1.call-done = bf16[80,640]{1,0:T(8,128)(2,1)} async-done(((bf16[1280,640]{1,0:T(8,128)(2,1)}), bf16[80,640]{1,0:T(8,128)(2,1)}) %reduce-scatter.11.cloned.1.call-update) | async-done | bytes 102416 | tf_op jit(solution)/shard_map/reduce_scatter | solution.py:263
  720.4 66.9 %reduce-scatter.19.cloned.1.call-done = bf16[80,640]{1,0:T(8,128)(2,1)} async-done(((bf16[1280,640]{1,0:T(8,128)(2,1)}), bf16[80,640]{1,0:T(8,128)(2,1)}) %reduce-scatter.19.cloned.1.call-update) | async-done | bytes 102416 | tf_op jit(solution)/shard_map/reduce_scatter | solution.py:275
  787.3 66.7 %reduce-scatter.23.cloned.1.call-done = bf16[80,640]{1,0:T(8,128)(2,1)} async-done(((bf16[1280,640]{1,0:T(8,128)(2,1)}), bf16[80,640]{1,0:T(8,128)(2,1)}) %reduce-scatter.23.cloned.1.call-update) | async-done | bytes 102416 | tf_op jit(solution)/shard_map/reduce_scatter | solution.py:281
  854.0 66.7 %reduce-scatter.25.cloned.1.call-done = bf16[40,1280]{1,0:T(8,128)(2,1)} async-done(((bf16[640,1280]{1,0:T(8,128)(2,1)}), bf16[40,1280]{1,0:T(8,128)(2,1)}) %reduce-scatter.25.cloned.1.call-update) | async-done | bytes 102416 | tf_op jit(solution)/shard_map/reduce_scatter | solution.py:284
  920.7 67.0 %reduce-scatter.15.cloned.1.call-done = bf16[80,640]{1,0:T(8,128)(2,1)} async-done(((bf16[1280,640]{1,0:T(8,128)(2,1)}), bf16[80,640]{1,0:T(8,128)(2,1)}) %reduce-scatter.15.cloned.1.call-update) | async-done | bytes 102416 | tf_op jit(solution)/shard_map/reduce_scatter | solution.py:269
  987.7 66.4 %reduce-scatter.13.cloned.1.call-done = bf16[80,640]{1,0:T(8,128)(2,1)} async-done(((bf16[1280,640]{1,0:T(8,128)(2,1)}), bf16[80,640]{1,0:T(8,128)(2,1)}) %reduce-scatter.13.cloned.1.call-update) | async-done | bytes 102416 | tf_op jit(solution)/shard_map/reduce_scatter | solution.py:266
  1054.2 2.7 fusion.100
  1060.7 167.6 %all-reduce.9.cloned.1.call-done = (bf16[80,640]{1,0:T(8,128)(2,1)}, bf16[80,640]{1,0:T(8,128)(2,1)}, bf16[80,640]{1,0:T(8,128)(2,1)}, bf16[40,1280]{1,0:T(8,128...) async-done(((bf16[80,640]{1,0:T(8,128)(2,1)}, bf16[80,640]{1,0:T(8,128)(2,1)}, ...) | async-done | bytes 819216 | tf_op jit(solution)/shard_map/psum | solution.py:289
  (214 shorter events, 79.0 us)
Async XLA Ops:
  7.2 40.6 %copy-start = (bf16[1,6,1280]{2,1,0:T(8,128)(2,1)S(1)}, bf16[1,6,1280]{2,1,0:T(8,128)(2,1)}, u32[]{:S(2)}) copy-start(bf16[1,6,1280]{2,1,0:T(8,128)(2,1)} %param.12) | copy-start | bytes 46084
  7.2 6.7 copy-start.1
  7.2 40.5 %all-gather.15.cloned.1.call-start = ((), (), s32[]{:S(2)}) async-start(), calls=%async_computation.18 | async-start | bytes 1740800 | tf_op jit(solution)/shard_map/all_gather | solution.py:122
  7.9 77.3 %all-gather.13.cloned.1.call-start = ((), (), s32[]{:S(2)}) async-start(), calls=%async_computation.17 | async-start | bytes 1740800 | tf_op jit(solution)/shard_map/all_gather | solution.py:121
  8.7 114.0 %all-gather.11.cloned.1.call-start = ((), (), s32[]{:S(2)}) async-start(), calls=%async_computation.16 | async-start | bytes 1740800 | tf_op jit(solution)/shard_map/all_gather | solution.py:123
  9.4 150.7 %all-gather.17.cloned.1.call-start = ((), (), s32[]{:S(2)}) async-start(), calls=%async_computation.19 | async-start | bytes 1740800 | tf_op jit(solution)/shard_map/all_gather | solution.py:124
  10.0 187.5 %all-gather.21.cloned.1.call-start = ((), (), s32[]{:S(2)}) async-start(), calls=%async_computation.21 | async-start | bytes 1740800 | tf_op jit(solution)/shard_map/all_gather | solution.py:125
  10.6 224.3 %all-gather.23.cloned.1.call-start = ((), (), s32[]{:S(2)}) async-start(), calls=%async_computation.22 | async-start | bytes 1740800 | tf_op jit(solution)/shard_map/all_gather | solution.py:126
  11.2 261.3 %all-gather.19.cloned.1.call-start = ((), (), s32[]{:S(2)}) async-start(), calls=%async_computation.20 | async-start | bytes 1740800 | tf_op jit(solution)/shard_map/all_gather | solution.py:127
  11.9 298.1 %all-gather.25.cloned.1.call-start = ((), (), s32[]{:S(2)}) async-start(), calls=%async_computation.23 | async-start | bytes 1740800 | tf_op jit(solution)/shard_map/all_gather | solution.py:128
  47.7 19.2 %copy-start.4 = (bf16[1280,640]{1,0:T(8,128)(2,1)S(1)}, bf16[1280,640]{1,0:T(8,128)(2,1)}, u32[]{:S(2)}) copy-start(bf16[1280,640]{1,0:T(8,128)(2,1)} %all-gather.15.cloned.1.call-done) | copy-start | bytes 4915204
  67.9 74.0 %copy-start.25 = (bf16[2,192,640]{1,2,0:T(8,128)(2,1)}, bf16[2,192,640]{1,2,0:T(8,128)(2,1)S(1)}, u32[]{:S(2)}) copy-start(bf16[2,192,640]{1,2,0:T(8,128)(2,1)S(1)} %copy.90) | copy-start | bytes 1474564
  122.7 20.4 %copy-start.2 = (bf16[1280,640]{1,0:T(8,128)(2,1)S(1)}, bf16[1280,640]{1,0:T(8,128)(2,1)}, u32[]{:S(2)}) copy-start(bf16[1280,640]{1,0:T(8,128)(2,1)} %all-gather.11.cloned.1.call-done) | copy-start | bytes 4915204
  144.1 2.0 copy-start.26
  146.2 16.1 %copy-start.30 = (bf16[2,4,160,96]{3,2,1,0:T(8,128)(2,1)}, bf16[2,4,160,96]{3,2,1,0:T(8,128)(2,1)S(1)}, u32[]{:S(2)}) copy-start(bf16[2,4,160,96]{3,2,1,0:T(8,128)(2,1)S(1)} %convolution_convert_fusion.11) | copy-start | bytes 737284
  200.4 37.4 %all-to-all-start.1 = ((bf16[2,96,640]{2,0,1:T(2,128)(2,1)}), bf16[2,96,640]{2,0,1:T(2,128)(2,1)S(1)}, u32[]{:S(2)}, u32[]{:S(2)}) async-start(bf16[2,96,640]{2,0,1:T(2,128)(2,1)} %copy.95), calls=%async_computation.1 | async-start | bytes 491520 | tf_op jit(solution)/shard_map/all_to_all | solution.py:166
  237.8 37.5 %all-to-all-start.2 = ((bf16[2,96,640]{2,0,1:T(2,128)(2,1)}), bf16[2,96,640]{2,0,1:T(2,128)(2,1)S(1)}, u32[]{:S(2)}, u32[]{:S(2)}) async-start(bf16[2,96,640]{2,0,1:T(2,128)(2,1)} %copy.97), calls=%async_computation.2 | async-start | bytes 491520 | tf_op jit(solution)/shard_map/all_to_all | solution.py:167
  242.6 67.4 %copy-start.12 = (bf16[1,2,96,1280]{3,2,1,0:T(8,128)(2,1)S(1)}, bf16[1,2,96,1280]{3,2,1,0:T(8,128)(2,1)}, u32[]{:S(2)}) copy-start(bf16[1,2,96,1280]{3,2,1,0:T(8,128)(2,1)} %param.13) | copy-start | bytes 1474564
  275.4 41.9 %all-to-all-start = ((bf16[2,96,640]{2,0,1:T(2,128)(2,1)}), bf16[2,96,640]{2,0,1:T(2,128)(2,1)}, u32[]{:S(2)}, u32[]{:S(2)}) async-start(bf16[2,96,640]{2,0,1:T(2,128)(2,1)} %copy.93), calls=%async_computation | async-start | bytes 491520 | tf_op jit(solution)/shard_map/all_to_all | solution.py:168
  317.3 11.7 all-to-all-start.4
  325.8 7.0 copy-start.28
  327.4 0.8 copy-start.39
  339.7 13.2 %all-to-all-start.6 = ((bf16[32,6,640]{2,1,0:T(8,128)(2,1)}), bf16[32,6,640]{2,1,0:T(8,128)(2,1)S(1)}, u32[]{:S(2)}, u32[]{:S(2)}) async-start(bf16[32,6,640]{2,1,0:T(8,128)(2,1)} %reshape.400), calls=%async_computation.6 | async-start | bytes 655360 | tf_op jit(solution)/shard_map/all_to_all | solution.py:194
  353.0 0.7 copy-start.20
  353.7 12.5 %all-to-all-start.5 = ((bf16[32,6,640]{2,1,0:T(8,128)(2,1)}), bf16[32,6,640]{2,1,0:T(8,128)(2,1)S(1)}, u32[]{:S(2)}, u32[]{:S(2)}) async-start(bf16[32,6,640]{2,1,0:T(8,128)(2,1)} %reshape.399), calls=%async_computation.5 | async-start | bytes 655360 | tf_op jit(solution)/shard_map/all_to_all | solution.py:191
  366.1 0.7 copy-start.17
  366.9 12.9 %all-to-all-start.7 = ((bf16[32,6,640]{2,1,0:T(8,128)(2,1)}), bf16[32,6,640]{2,1,0:T(8,128)(2,1)S(1)}, u32[]{:S(2)}, u32[]{:S(2)}) async-start(bf16[32,6,640]{2,1,0:T(8,128)(2,1)} %reshape.401), calls=%async_computation.7 | async-start | bytes 655360 | tf_op jit(solution)/shard_map/all_to_all | solution.py:201
  371.5 149.6 %all-reduce.7.cloned.1.call-start = ((), (), s32[]{:S(2)}) async-start(), calls=%async_computation.32 | async-start | bytes 655360
  375.5 2.5 copy-start.21
  375.5 3.4 copy-start.18
  379.8 2.7 copy-start.15
  379.8 2.7 copy-start.10
  379.8 2.7 copy-start.31
  382.5 1.4 copy-start.11
  384.8 1.4 copy-start.9
  386.2 15.4 %copy-start.7 = (bf16[2,96,1280]{2,1,0:T(8,128)(2,1)}, bf16[2,96,1280]{2,1,0:T(8,128)(2,1)S(1)}, u32[]{:S(2)}) copy-start(bf16[2,96,1280]{2,1,0:T(8,128)(2,1)S(1)} %add_convert_fusion) | copy-start | bytes 1474564
  392.4 2.5 copy-start.32
  401.5 185.3 %reduce-scatter.17.cloned.1.call-start = ((), (), s32[]{:S(2)}) async-start(), calls=%async_computation.27 | async-start | bytes 1740800 | tf_op jit(solution)/shard_map/reduce_scatter | solution.py:272
  401.6 3.1 copy-start.22
  404.4 249.3 %reduce-scatter.21.cloned.1.call-start = ((), (), s32[]{:S(2)}) async-start(), calls=%async_computation.29 | async-start | bytes 1740800 | tf_op jit(solution)/shard_map/reduce_scatter | solution.py:278
  407.0 313.4 %reduce-scatter.11.cloned.1.call-start = ((), (), s32[]{:S(2)}) async-start(), calls=%async_computation.24 | async-start | bytes 1740800 | tf_op jit(solution)/shard_map/reduce_scatter | solution.py:263
  412.7 3.0 copy-start.19
  415.7 371.6 %reduce-scatter.19.cloned.1.call-start = ((), (), s32[]{:S(2)}) async-start(), calls=%async_computation.28 | async-start | bytes 1740800 | tf_op jit(solution)/shard_map/reduce_scatter | solution.py:275
  416.1 2.0 copy-start.16
  418.0 436.0 %reduce-scatter.23.cloned.1.call-start = ((), (), s32[]{:S(2)}) async-start(), calls=%async_computation.30 | async-start | bytes 1740800 | tf_op jit(solution)/shard_map/reduce_scatter | solution.py:281
  419.2 3.0 copy-start.29
  422.1 498.6 %reduce-scatter.25.cloned.1.call-start = ((), (), s32[]{:S(2)}) async-start(), calls=%async_computation.31 | async-start | bytes 1740800 | tf_op jit(solution)/shard_map/reduce_scatter | solution.py:284
  440.2 1.9 copy-start.38
  442.1 545.6 %reduce-scatter.15.cloned.1.call-start = ((), (), s32[]{:S(2)}) async-start(), calls=%async_computation.26 | async-start | bytes 1740800 | tf_op jit(solution)/shard_map/reduce_scatter | solution.py:269
  525.0 529.1 %reduce-scatter.13.cloned.1.call-start = ((), (), s32[]{:S(2)}) async-start(), calls=%async_computation.25 | async-start | bytes 1740800 | tf_op jit(solution)/shard_map/reduce_scatter | solution.py:266
  526.2 0.8 copy-start.23
  526.2 1.0 copy-start.34
  529.2 1.4 copy-start.27
  529.2 699.1 %all-reduce.9.cloned.1.call-start = ((), (), s32[]{:S(2)}) async-start(), calls=%async_computation.33 | async-start | bytes 1638400 | tf_op jit(solution)/shard_map/psum | solution.py:289
  529.5 2.8 copy-start.5
  529.5 2.8 copy-start.24
  532.3 1.4 copy-start.3
  1054.2 2.7 copy-start.14
  1054.2 2.9 copy-start.8
  1057.1 1.4 copy-start.6
  1057.1 1.4 copy-start.35
  1058.5 0.9 copy-start.33
  1228.3 9.6 copy-start.37
  1228.3 10.3 copy-start.36
  (1 other events, 0.7 us)
Sparse Core Ops, SparseCore 0:
  9.9 37.8 all-gather.14
  49.6 35.6 all-gather.12
  87.1 35.5 all-gather.10
  124.4 35.6 all-gather.16
  161.8 35.6 all-gather.20
  199.2 35.6 all-gather.22
  236.8 35.6 all-gather.18
  274.3 35.6 all-gather.24
  401.6 119.4 all-reduce.6
  523.5 63.2 reduce-scatter.16
  589.4 64.2 reduce-scatter.20
  656.1 64.2 reduce-scatter.10
  723.0 64.2 reduce-scatter.18
  789.7 64.2 reduce-scatter.22
  856.4 64.2 reduce-scatter.24
  923.1 64.5 reduce-scatter.14
  990.1 64.0 reduce-scatter.12
  1057.2 170.9 all-reduce.8
where the time goes:
time: 1260 us; the launch traced here: 1250 us
  waiting for transfers between devices  991 us (79%)
  matrix products  81.4 us (6%)
  local copies, waits for them, and re-layouts  51.1 us (4%)
  blocking collectives  47.6 us (4%)
  starting transfers between devices  36.3 us (3%)
  other arithmetic  23.1 us (2%)
  between operations  15.9 us (1%)
    psum x1, waiting for transfers between devices, per_device(): lax.psum(share_sq.astype(jnp.bfloat16), 'clip').astype(jnp.float32)  168 us
    unnamed x19, waiting for transfers between devices  79.4 us
    reduce_scatter x1, waiting for transfers between devices, per_device(): lax.psum_scatter(term_sv.astype(jnp.bfloat16), 'frame', scatter_dimension...  67 us
    reduce_scatter x1, waiting for transfers between devices, per_device(): lax.psum_scatter(term_tk.astype(jnp.bfloat16), 'frame', scatter_dimension...  66.9 us
    reduce_scatter x1, waiting for transfers between devices, per_device(): lax.psum_scatter(term_tq.astype(jnp.bfloat16), 'frame', scatter_dimension...  66.9 us
    reduce_scatter x1, waiting for transfers between devices, per_device(): lax.psum_scatter(term_sq.astype(jnp.bfloat16), 'frame', scatter_dimension...  66.7 us
    reduce_scatter x1, waiting for transfers between devices, per_device(): lax.psum_scatter(term_tv.astype(jnp.bfloat16), 'frame', scatter_dimension...  66.7 us
    reduce_scatter x1, waiting for transfers between devices, per_device(): lax.psum_scatter(term_to.astype(jnp.bfloat16), 'frame', scatter_dimension...  66.7 us
  transfers between devices with their start and end apart: 25, of which 20 were waited for; matrix products, arithmetic and copies ran while one was open for 9% of the time, Pallas kernels for 0%

commit v1 on v0

v1 whole, which is shorter than its diff:
```python
import math

import jax
import jax.numpy as jnp
from jax import lax
from jax.experimental import pallas as pl
from jax.experimental.pallas import tpu as pltpu
from jax.sharding import PartitionSpec as P


MESH = pl.DeviceIdType.MESH
ANY = pl.BlockSpec(memory_space=pl.ANY)
VM = pl.BlockSpec(memory_space=pltpu.VMEM)


class Place:
    def __init__(self):
        clip, frame = lax.axis_index("clip"), lax.axis_index("frame")
        self.clip, self.frame = clip, frame
        self.x, self.zh = lax.rem(clip, 4), lax.div(clip, 4)
        self.y, self.zl, self.core = lax.div(frame, 4), lax.rem(lax.div(frame, 2), 2), lax.rem(frame, 2)
        self.parity = lax.rem(self.x, 2)
        self.sibling = (clip, frame + 1 - 2 * self.core)

    def along_y(self, step):
        return (self.clip, lax.rem(self.y + 4 + step, 4) * 4 + self.zl * 2 + self.core)

    def along_x(self, step):
        return (self.zh * 4 + lax.rem(self.x + 4 + step, 4), self.frame)

    def along_z(self, step):
        far = lax.rem(self.zh * 2 + self.zl + 8 + step, 8)
        return (lax.div(far, 2) * 4 + self.x, self.y * 4 + lax.rem(far, 2) * 2 + self.core)

    def along_zh(self, step):
        return (lax.rem(self.zh + 4 + step, 4) * 4 + self.x, self.frame)

    def peer(self, step):
        return (self.clip, lax.rem(self.frame + step, 16))


def greet(devices):
    barrier = pltpu.get_barrier_semaphore()
    for device in devices:
        pl.semaphore_signal(barrier, inc=1, device_id=device, device_id_type=MESH)
    pl.semaphore_wait(barrier, len(devices))


def remote(src, dst, send, recv, device):
    return pltpu.make_async_remote_copy(
        src_ref=src, dst_ref=dst, send_sem=send, recv_sem=recv, device_id=device, device_id_type=MESH)


def shard_of(y, zl, core):
    return lax.rem(y + 8, 4) * 4 + zl * 2 + core


def gather_kernel(pack, ref8, full, refs, sib_s, sib_r, y_s, y_r, rel_s, rel_r, z_s, z_r, x_s, x_r, ref_s, ref_r, loc):
    at = Place()
    y, zl, core, p, me = at.y, at.zl, at.core, at.parity, at.frame
    greet([at.along_x(1), at.along_x(-1), at.along_z(1), at.along_z(-1)] + [at.peer(i) for i in range(1, 16)])
    sends = []

    def go(copy):
        copy.start()
        sends.append(copy)

    def pair(j):
        return pl.ds(2 * j, 2)

    steps = (1, -1)
    own = [[None] * 4 for _ in steps]
    for j in range(4):
        for s, step in enumerate(steps):
            own[s][j] = remote(pack.at[pair(j)], full.at[me, pair(j)], y_s.at[s, j], y_r.at[s, j], at.along_y(step))

    def z_copy(k, h, d, src):
        w = 4 * h + 2 * p + d
        return remote(src, full.at[shard_of(y + k, zl, core), w], z_s.at[k, h, d], z_r.at[k, h, d],
                      at.along_z(1 - 2 * d))

    sib_count = [0]

    def to_sibling(index, src, dst):
        go(remote(src, dst, sib_s.at[index], sib_r.at[index], at.sibling))

    for j in range(2):
        for s in range(2):
            go(own[s][j])
    for d in range(2):
        go(z_copy(0, 0, d, pack.at[2 * p + d]))
    for j in range(2, 4):
        for s in range(2):
            go(own[s][j])
    for d in range(2):
        go(z_copy(0, 1, d, pack.at[4 + 2 * p + d]))
    to_sibling(0, pack, full.at[me])
    keep = pltpu.make_async_copy(pack, full.at[me], loc.at[0])
    keep.start()
    keep_ref = pltpu.make_async_copy(ref8, refs.at[me], loc.at[1])
    keep_ref.start()
    for i in range(1, 16):
        go(remote(ref8, refs.at[me], ref_s.at[i], ref_r.at[i], at.peer(i)))

    def y_wait(s, j):
        src = shard_of(y - steps[s], zl, core)
        ref = full.at[src, pair(j)]
        remote(ref, ref, y_s.at[s, j], y_r.at[s, j], at.along_y(steps[s])).wait_recv()
        to_sibling(1 + s * 4 + j, ref, ref)
        if j % 2 == s:
            go(remote(ref, ref, rel_s.at[j], rel_r.at[j], at.along_y(steps[s])))

    def rel_wait(j):
        ref = full.at[shard_of(y + 2, zl, core), pair(j)]
        remote(ref, ref, rel_s.at[j], rel_r.at[j], at.along_y(1)).wait_recv()
        to_sibling(9 + j, ref, ref)

    def z_send(k, h):
        for d in range(2):
            go(z_copy(k, h, d, full.at[shard_of(y + k, zl, core), 4 * h + 2 * p + d]))

    def z_wait(k, h):
        for d in range(2):
            ref = full.at[shard_of(y + k, 1 - zl, core), 4 * h + 2 * p + d]
            remote(ref, ref, z_s.at[k, h, d], z_r.at[k, h, d], at.along_z(1)).wait_recv()
            go(remote(ref, ref, x_s.at[k, h, d], x_r.at[k, h, d], at.along_x(1 - 2 * d)))
            to_sibling(13 + (k * 2 + h) * 2 + d, ref, ref)

    def x_wait(k, h):
        for d in range(2):
            ref = full.at[shard_of(y + k, 1 - zl, core), 4 * h + 2 * (1 - p) + d]
            remote(ref, ref, x_s.at[k, h, d], x_r.at[k, h, d], at.along_x(1)).wait_recv()
            to_sibling(29 + (k * 2 + h) * 2 + d, ref, ref)

    for h in range(2):
        for j in (2 * h, 2 * h + 1):
            for s in range(2):
                y_wait(s, j)
        z_send(1, h)
        z_send(3, h)
        z_wait(0, h)
        for j in (2 * h, 2 * h + 1):
            rel_wait(j)
        z_send(2, h)
        z_wait(1, h)
        z_wait(3, h)
        x_wait(0, h)
        z_wait(2, h)
        x_wait(1, h)
        x_wait(3, h)
        x_wait(2, h)

    other = 1 - core

    def sib_wait(index, ref):
        remote(ref, ref, sib_s.at[index], sib_r.at[index], at.sibling).wait_recv()

    sib_wait(0, full.at[shard_of(y, zl, other)])
    for s in range(2):
        for j in range(4):
            sib_wait(1 + s * 4 + j, full.at[shard_of(y - steps[s], zl, other), pair(j)])
    for j in range(4):
        sib_wait(9 + j, full.at[shard_of(y + 2, zl, other), pair(j)])
    for k in range(4):
        for h in range(2):
            for d in range(2):
                i = (k * 2 + h) * 2 + d
                dst = shard_of(y + k, 1 - zl, other)
                sib_wait(13 + i, full.at[dst, 4 * h + 2 * p + d])
                sib_wait(29 + i, full.at[dst, 4 * h + 2 * (1 - p) + d])
    for i in range(1, 16):
        ref = refs.at[lax.rem(me + 16 - i, 16)]
        remote(ref, ref, ref_s.at[i], ref_r.at[i], at.peer(i)).wait_recv()
    for copy in sends:
        copy.wait_send()
    keep.wait()
    keep_ref.wait()


def gather(pack, ref8):
    dma = pltpu.SemaphoreType.DMA
    return pl.pallas_call(
        gather_kernel,
        out_shape=(jax.ShapeDtypeStruct((16, 8, 80, 640), jnp.bfloat16),
                   jax.ShapeDtypeStruct((16, 8, 1280), jnp.bfloat16)),
        in_specs=[VM, VM],
        out_specs=(ANY, ANY),
        scratch_shapes=[dma((45,)), dma((45,)), dma((2, 4)), dma((2, 4)), dma((4,)), dma((4,)),
                        dma((4, 2, 2)), dma((4, 2, 2)), dma((4, 2, 2)), dma((4, 2, 2)), dma((16,)), dma((16,)),
                        dma((2,))],
        compiler_params=pltpu.CompilerParams(collective_id=0, has_side_effects=True),
        name="gather_weights",
    )(pack, ref8)

BF, F32 = jnp.bfloat16, jnp.float32
EPSILON = 1e-05
SCALE = 160 ** -0.5


def dot(a, b, ca=1, cb=0):
    return lax.dot_general(a, b, (((ca,), (cb,)), ((), ())), preferred_element_type=F32)


def stats(wide):
    offset = wide - jnp.mean(wide, -1, keepdims=True)
    inverse = lax.rsqrt(jnp.mean(offset * offset, -1, keepdims=True) + EPSILON)
    return offset * inverse, inverse


def stats_back(centred, inverse, g):
    first = jnp.mean(g, -1, keepdims=True)
    second = jnp.mean(g * centred, -1, keepdims=True)
    return inverse * (g - first - centred * second)


def iota(shape, dim):
    return lax.broadcasted_iota(jnp.int32, shape, dim)


def one_hot(hit):
    return jnp.where(hit, 1.0, 0.0).astype(BF)


def frame_pack():
    r, c = iota((256, 192), 0), iota((256, 192), 1)
    d, j = lax.shift_right_logical(r, 4), lax.bitwise_and(r, 15)
    a = jnp.where(j >= 6, 1, 0)
    return one_hot((j < 12) & (c == 90 * a + 6 * d + j))


def frame_unpack():
    c, r = iota((192, 256), 0), iota((192, 256), 1)
    d, j = lax.shift_right_logical(r, 4), lax.bitwise_and(r, 15)
    a = jnp.where(j >= 6, 1, 0)
    return one_hot((j < 12) & (c == 90 * a + 6 * d + j))


def token_unpack():
    m, r = iota((192, 256), 0), iota((192, 256), 1)
    t, f, a = lax.shift_right_logical(m, 5), lax.bitwise_and(lax.shift_right_logical(m, 1), 15), lax.bitwise_and(m, 1)
    return one_hot(r == 16 * f + 6 * a + t)


def token_pack():
    m, r = iota((256, 192), 1), iota((256, 192), 0)
    t, f, a = lax.shift_right_logical(m, 5), lax.bitwise_and(lax.shift_right_logical(m, 1), 15), lax.bitwise_and(m, 1)
    return one_hot(r == 16 * f + 6 * a + t)


def ref_unpack(rows, cols, swap=False):
    m, r = (iota((rows, cols), 0), iota((rows, cols), 1)) if not swap else (iota((rows, cols), 1), iota((rows, cols), 0))
    d, j = lax.shift_right_logical(r, 3), lax.bitwise_and(r, 7)
    return one_hot((j < 6) & (m == 6 * d + j))


def head_masks():
    lane = iota((1, 640), 1)
    return [(lane >= 160 * h) & (lane < 160 * (h + 1)) for h in range(4)]


def stack_heads(rows, masks):
    return jnp.concatenate([rows * one_hot(m) for m in masks], 0)


def merge_heads(stacked, masks):
    n = stacked.shape[0] // 4
    total = jnp.where(masks[0], stacked[:n], 0.0)
    for h in range(1, 4):
        total = jnp.where(masks[h], stacked[h * n:(h + 1) * n], total)
    return total


def softmax(stacked, keys, same=None):
    powers = jnp.exp(dot(stacked, keys, 1, 1) * SCALE)
    if same is not None:
        powers = jnp.where(same, powers, 0.0)
    return powers / jnp.sum(powers, -1, keepdims=True)


def score_back(probs, grads, values):
    dp = dot(grads, values, 1, 1)
    return (probs * (dp - jnp.sum(probs * dp, -1, keepdims=True)) * SCALE).astype(BF)


def wide_output(slot):
    wide = slot.astype(F32)
    left = wide[:, :40].reshape(640, 640).astype(BF)
    right = wide[:, 40:].reshape(640, 640).astype(BF)
    return left, right


def pack_output(left, right):
    return jnp.concatenate([left.reshape(16, 40, 640), right.reshape(16, 40, 640)], 1)


def store_term(dw, w, term):
    parts = term.reshape(4, 2, 2, 80, 640).astype(BF)
    for core in range(2):
        for zl in range(2):
            dw[core, zl, w] = parts[:, zl, core]


def exchange_start(at, src, dst, send, recv):
    copies = []
    for i in range(1, 16):
        to = lax.rem(at.frame + i, 16)
        copy = remote(src.at[pl.ds(pl.multiple_of(16 * to, 16), 16)],
                      dst.at[pl.ds(pl.multiple_of(16 * at.frame, 16), 16)], send.at[i], recv.at[i], at.peer(i))
        copy.start()
        copies.append(copy)
    own = pl.ds(pl.multiple_of(16 * at.frame, 16), 16)
    dst[own, :] = src[own, :]
    return copies


def load(src, dst, sem):
    copy = pltpu.make_async_copy(src, dst, sem)
    copy.start()
    return copy


def space_kernel(frames, refs, og, full, h1_o, qkv_o, rkv_o, o_o, h1r, ogr, wts, buf_a, buf_b, wsem, s_s, r_s):
    at = Place()
    loads = [load(full.at[:, i], wts.at[i], wsem.at[i]) for i in range(4)]
    greet([at.peer(i) for i in range(1, 16)])
    pack = frame_pack()
    buf_a[...] = dot(pack, og[...]).astype(BF)
    copies = exchange_start(at, buf_a, ogr, s_s.at[0], r_s.at[0])
    masks = head_masks()
    wide = frames[...].astype(F32)
    n1 = stats(wide)[0].astype(BF)
    ref = dot(ref_unpack(96, 128), refs[...]).astype(BF)
    loads[0].wait()
    q = dot(n1, wts[0].reshape(1280, 640)).astype(BF)
    loads[1].wait()
    w = wts[1].reshape(1280, 640)
    k, rk = dot(n1, w).astype(BF), dot(ref, w).astype(BF)
    loads[2].wait()
    w = wts[2].reshape(1280, 640)
    v, rv = dot(n1, w).astype(BF), dot(ref, w).astype(BF)
    for i, part in enumerate((q, k, v)):
        qkv_o[i] = part
    rkv_o[0] = rk
    rkv_o[1] = rv
    outs = []
    for a in range(2):
        rows = slice(96 * a, 96 * a + 96)
        keys = jnp.concatenate([k[rows], rk], 0)
        values = jnp.concatenate([v[rows], rv], 0)
        probs = softmax(stack_heads(q[rows], masks), keys).astype(BF)
        outs.append(merge_heads(dot(probs, values), masks))
    o = jnp.concatenate(outs, 0).astype(BF)
    o_o[...] = o
    loads[3].wait()
    left, right = wide_output(wts[3])
    h1 = (wide + jnp.concatenate([dot(o, left), dot(o, right)], 1)).astype(BF)
    h1_o[...] = h1
    buf_b[...] = dot(pack, h1).astype(BF)
    copies += exchange_start(at, buf_b, h1r, s_s.at[1], r_s.at[1])
    for copy in copies:
        copy.wait()


def space(frames, refs, og, full):
    dma = pltpu.SemaphoreType.DMA
    s = jax.ShapeDtypeStruct
    return pl.pallas_call(
        space_kernel,
        out_shape=(s((192, 1280), BF), s((3, 192, 640), BF), s((2, 96, 640), BF), s((192, 640), BF),
                   s((256, 1280), BF), s((256, 1280), BF)),
        in_specs=[VM, VM, VM, ANY],
        out_specs=(VM,) * 6,
        scratch_shapes=[pltpu.VMEM((4, 16, 80, 640), BF), pltpu.VMEM((256, 1280), BF), pltpu.VMEM((256, 1280), BF),
                        dma((4,)), dma((2, 16)), dma((2, 16))],
        compiler_params=pltpu.CompilerParams(collective_id=1, has_side_effects=True, vmem_limit_bytes=60 << 20),
        name="space_forward",
    )(frames, refs, og, full)


def time_kernel(h1r, ogr, table, full, back, dw, wts, buf, wsem, s_s, r_s):
    at = Place()
    loads = [load(full.at[:, 4 + i], wts.at[i], wsem.at[i]) for i in range(4)]
    greet([at.peer(i) for i in range(1, 16)])
    masks = head_masks()
    unpack = token_unpack()
    h1 = dot(unpack, h1r[...])
    og = dot(unpack, ogr[...]).astype(BF)
    centred, inverse = stats(h1)
    n2 = (centred + jnp.concatenate([table[...]] * 6, 0)).astype(BF)
    parts = []
    for i in range(3):
        loads[i].wait()
        parts.append(dot(n2, wts[i].reshape(1280, 640)).astype(BF))
    q, k, v = parts
    r, c = iota((768, 192), 0), iota((768, 192), 1)
    r = jnp.where(r >= 384, r - 384, r)
    r = jnp.where(r >= 192, r - 192, r)
    same = lax.shift_right_logical(r, 5) == lax.shift_right_logical(c, 5)
    qs = stack_heads(q, masks)
    probs = softmax(qs, k, same)
    pb = probs.astype(BF)
    o2 = merge_heads(dot(pb, v), masks).astype(BF)
    loads[3].wait()
    left, right = wide_output(wts[3])
    go = (dot(og[:, :640], left, 1, 1) + dot(og[:, 640:], right, 1, 1)).astype(BF)
    gs = stack_heads(go, masks)
    eb = score_back(probs, gs, v)
    gq = merge_heads(dot(eb, k), masks).astype(BF)
    gk = dot(eb, qs, 0, 0).astype(BF)
    gv = dot(pb, gs, 0, 0).astype(BF)
    grads = (gq, gk, gv)
    gn = dot(gq, wts[0].reshape(1280, 640), 1, 1)
    for i in (1, 2):
        gn = gn + dot(grads[i], wts[i].reshape(1280, 640), 1, 1)
    gh = (og.astype(F32) + stats_back(centred, inverse, gn)).astype(BF)
    pack = token_pack()
    buf[:, :1280] = dot(pack, gh).astype(BF)
    buf[:, 1280:] = dot(pack, o2).astype(BF)
    copies = exchange_start(at, buf, back, s_s, r_s)
    for i in range(3):
        store_term(dw, i, dot(n2, grads[i], 0, 0))
    store_term(dw, 3, pack_output(dot(o2, og[:, :640], 0, 0), dot(o2, og[:, 640:], 0, 0)))
    for copy in copies:
        copy.wait()


def temporal(h1r, ogr, table, full):
    dma = pltpu.SemaphoreType.DMA
    s = jax.ShapeDtypeStruct
    return pl.pallas_call(
        time_kernel,
        out_shape=(s((256, 1920), BF), s((2, 2, 4, 4, 80, 640), BF)),
        in_specs=[VM, VM, VM, ANY],
        out_specs=(VM, VM),
        scratch_shapes=[pltpu.VMEM((4, 16, 80, 640), BF), pltpu.VMEM((256, 1920), BF),
                        dma((4,)), dma((16,)), dma((16,))],
        compiler_params=pltpu.CompilerParams(collective_id=2, has_side_effects=True, vmem_limit_bytes=60 << 20),
        name="time_both",
    )(h1r, ogr, table, full)


def back_kernel(backr, frames, refs, h1, qkv, rkv, o_in, full, out_o, fg_o, dw, gr_o, wts, wsem):
    order = (7, 3, 0, 1, 2)
    loads = {i: load(full.at[:, i], wts.at[n], wsem.at[n]) for n, i in enumerate(order)}
    masks = head_masks()
    unpack = frame_unpack()
    gh = dot(unpack, backr[:, :1280]).astype(BF)
    o2 = dot(unpack, backr[:, 1280:]).astype(BF)
    loads[7].wait()
    left, right = wide_output(wts[0])
    out_o[...] = (h1[...].astype(F32) + jnp.concatenate([dot(o2, left), dot(o2, right)], 1)).astype(BF)
    loads[3].wait()
    left, right = wide_output(wts[1])
    go = (dot(gh[:, :640], left, 1, 1) + dot(gh[:, 640:], right, 1, 1)).astype(BF)
    rk, rv = rkv[0], rkv[1]
    gq, gk, gv = [], [], []
    grk = grv = None
    for a in range(2):
        rows = slice(96 * a, 96 * a + 96)
        keys = jnp.concatenate([qkv[1, rows], rk], 0)
        values = jnp.concatenate([qkv[2, rows], rv], 0)
        qs = stack_heads(qkv[0, rows], masks)
        gs = stack_heads(go[rows], masks)
        probs = softmax(qs, keys)
        eb = score_back(probs, gs, values)
        gq.append(merge_heads(dot(eb, keys), masks))
        gkeys = dot(eb, qs, 0, 0)
        gvalues = dot(probs.astype(BF), gs, 0, 0)
        gk.append(gkeys[:96])
        gv.append(gvalues[:96])
        grk = gkeys[96:] if grk is None else grk + gkeys[96:]
        grv = gvalues[96:] if grv is None else grv + gvalues[96:]
    gq, gk, gv = (jnp.concatenate(g, 0).astype(BF) for g in (gq, gk, gv))
    grk, grv = grk.astype(BF), grv.astype(BF)
    spread = ref_unpack(128, 96, True)
    gr_o[:, :640] = dot(spread, grk).astype(BF)
    gr_o[:, 640:] = dot(spread, grv).astype(BF)
    ref = dot(ref_unpack(96, 128), refs[...]).astype(BF)
    centred, inverse = stats(frames[...].astype(F32))
    n1 = centred.astype(BF)
    gn = None
    for n, (i, g) in enumerate(((0, gq), (1, gk), (2, gv))):
        loads[i].wait()
        term = dot(g, wts[2 + n].reshape(1280, 640), 1, 1)
        gn = term if gn is None else gn + term
    fg_o[...] = (gh.astype(F32) + stats_back(centred, inverse, gn)).astype(BF)
    store_term(dw, 0, dot(n1, gq, 0, 0))
    store_term(dw, 1, dot(n1, gk, 0, 0) + dot(ref, grk, 0, 0))
    store_term(dw, 2, dot(n1, gv, 0, 0) + dot(ref, grv, 0, 0))
    o = o_in[...]
    store_term(dw, 3, pack_output(dot(o, gh[:, :640], 0, 0), dot(o, gh[:, 640:], 0, 0)))


def back(backr, frames, refs, h1, qkv, rkv, o, full):
    dma = pltpu.SemaphoreType.DMA
    s = jax.ShapeDtypeStruct
    return pl.pallas_call(
        back_kernel,
        out_shape=(s((192, 1280), BF), s((192, 1280), BF), s((2, 2, 4, 4, 80, 640), BF), s((128, 1280), BF)),
        in_specs=[VM] * 7 + [ANY],
        out_specs=(VM,) * 4,
        scratch_shapes=[pltpu.VMEM((5, 16, 80, 640), BF), dma((5,))],
        compiler_params=pltpu.CompilerParams(vmem_limit_bytes=60 << 20),
        name="space_backward",
    )(backr, frames, refs, h1, qkv, rkv, o, full)


def add(*parts):
    total = parts[0].astype(F32)
    for part in parts[1:]:
        total = total + part.astype(F32)
    return total


def reduce_kernel(dws, dwt, gr, full, tot_sq, tot_sk, tot_sv, tot_so, tot_tq, tot_tk, tot_tv, tot_to, rg,
                  g, r0, rx, rz, ry1, ry2, pm, rax1, rax2, rq, fin, rgr, wts,
                  l_m, c_s, c_r, x_s, x_r, z_s, z_r, y1_s, y1_r, y2_s, y2_r,
                  a1_s, a1_r, a2_s, a2_r, q_s, q_r, g_s, g_r, gg_s, gg_r, e_s, e_r, w_m):
    at = Place()
    y, zl, p, x, zh, me = at.y, at.zl, at.parity, at.x, at.zh, at.frame
    core, oz = at.core, 1 - at.zl
    wloads = [load(full.at[:, 1 + i], wts.at[i], w_m.at[i]) for i in range(2)]
    halves = (dws, dwt)
    locals_ = {}
    for h in (1, 0):
        for a, zz in enumerate((oz, zl)):
            for w in range(4):
                locals_[h, a, w] = load(halves[h].at[core, zz, w], g.at[h, a, w], l_m.at[h, a, w])
    greet([at.peer(i) for i in range(1, 16)] + [at.along_x(1), at.along_x(-1), at.along_z(1), at.along_z(-1),
                                                at.along_zh(1), at.along_zh(-1), at.along_zh(2)])
    sends = []

    def go(copy):
        copy.start()
        sends.append(copy)
        return copy

    cross = {}
    for h in (1, 0):
        for a, zz in enumerate((oz, zl)):
            for w in range(4):
                cross[h, a, w] = go(remote(halves[h].at[1 - core, zz, w], r0.at[h, a, w], c_s.at[h, a, w],
                                           c_r.at[h, a, w], at.sibling))
    refs = []
    for i in range(1, 16):
        to = lax.rem(me + i, 16)
        refs.append(go(remote(gr.at[to], rgr.at[me], e_s.at[i], e_r.at[i], at.peer(i))))
    rgr[me] = gr[me]

    def rem4(v):
        return lax.rem(v + 8, 4)

    def chain(h):
        for a in range(2):
            for w in range(4):
                locals_[h, a, w].wait()
                cross[h, a, w].wait_recv()
                g[h, a, w] = add(g[h, a, w], r0[h, a, w]).astype(BF)
            if a == 0:
                xs = [go(remote(g.at[h, 0, 2 * (1 - p) + d], rx.at[h, d], x_s.at[h, d], x_r.at[h, d],
                                at.along_x(2 * d - 1))) for d in range(2)]
        yield
        zs = []
        for d in range(2):
            xs[d].wait_recv()
            w = 2 * p + d
            g[h, 0, w] = add(g[h, 0, w], rx[h, d]).astype(BF)
            zs.append(go(remote(g.at[h, 0, w], rz.at[h, d], z_s.at[h, d], z_r.at[h, d], at.along_z(2 * d - 1))))
        yield
        for d in range(2):
            zs[d].wait_recv()
            w = 2 * p + d
            g[h, 1, w] = add(g[h, 1, w], rz[h, d]).astype(BF)
        y1 = [go(remote(g.at[h, 1, w, rem4(y + 2)], ry1.at[h, w], y1_s.at[h, w], y1_r.at[h, w],
                        at.along_y(-1 if w < 2 else 1))) for w in range(4)]
        yield
        y2 = {}
        for w in range(4):
            y1[w].wait_recv()
            on = rem4(y + (-1 if w < 2 else 1))
            g[h, 1, w, on] = add(g[h, 1, w, on], ry1[h, w]).astype(BF)
            for s, step in enumerate((1, -1)):
                y2[s, w] = go(remote(g.at[h, 1, w, rem4(y + step)], ry2.at[s, h, w], y2_s.at[s, h, w],
                                     y2_r.at[s, h, w], at.along_y(step)))
        yield
        for w in range(4):
            y2[0, w].wait_recv()
            y2[1, w].wait_recv()
            pm[h, w] = add(g[h, 1, w, y], ry2[0, h, w], ry2[1, h, w]).astype(BF)
        low, high = pl.ds(0, 48), pl.ds(48, 32)
        far = rem4(x + 2)
        a1 = [go(remote(pm.at[h, far, part], rax1.at[h, part], a1_s.at[h, s], a1_r.at[h, s], at.along_x(step)))
              for s, (step, part) in enumerate(((1, low), (-1, high)))]
        yield
        for s, (step, part) in enumerate(((1, low), (-1, high))):
            a1[s].wait_recv()
            on = rem4(x + step)
            pm[h, on, part] = add(pm[h, on, part], rax1[h, part]).astype(BF)
        a2 = [go(remote(pm.at[h, rem4(x + step)], rax2.at[s, h], a2_s.at[s, h], a2_r.at[s, h], at.along_x(step)))
              for s, step in enumerate((1, -1))]
        yield
        for copy in a2:
            copy.wait_recv()
        rq[h, zh] = add(pm[h, x], rax2[0, h], rax2[1, h]).astype(BF)
        qs = [go(remote(rq.at[h, zh], rq.at[h, zh], q_s.at[h, i], q_r.at[h, i], at.along_zh(step)))
              for i, step in enumerate((2, 1, -1))]
        yield
        for i, step in enumerate((2, 1, -1)):
            ref = rq.at[h, rem4(zh - step)]
            remote(ref, ref, q_s.at[h, i], q_r.at[h, i], at.along_zh(step)).wait_recv()
        fin[h, x] = add(rq[h, 0], rq[h, 1], rq[h, 2], rq[h, 3]).astype(BF)
        for s, step in enumerate((1, -1)):
            go(remote(fin.at[h, x], fin.at[h, x], g_s.at[h, s], g_r.at[h, s], at.along_x(step)))
        yield
        for s, (step, part) in enumerate(((1, low), (-1, high))):
            ref = fin.at[h, rem4(x - step)]
            remote(ref, ref, g_s.at[h, s], g_r.at[h, s], at.along_x(step)).wait_recv()
            ref = fin.at[h, rem4(x - step), part]
            go(remote(ref, ref, gg_s.at[h, s], gg_r.at[h, s], at.along_x(step)))
        yield
        for s, (step, part) in enumerate(((1, low), (-1, high))):
            ref = fin.at[h, rem4(x + 2), part]
            remote(ref, ref, gg_s.at[h, s], gg_r.at[h, s], at.along_x(step)).wait_recv()
        outs = (tot_sq, tot_sk, tot_sv, tot_so) if h == 0 else (tot_tq, tot_tk, tot_tv, tot_to)
        for w in range(3):
            outs[w][...] = fin[h, w].astype(F32)
        wide = fin[h, 3].astype(F32)
        outs[3][:, :640] = wide[:40]
        outs[3][:, 640:] = wide[40:]

    first, second = chain(1), chain(0)
    live = [first]
    step = 0
    while live:
        for c in list(live):
            try:
                next(c)
            except StopIteration:
                live.remove(c)
        step += 1
        if step == 1:
            live.append(second)
            next(second)
        if step == 2:
            for i in range(1, 16):
                ref = rgr.at[lax.rem(me + 16 - i, 16)]
                remote(ref, ref, e_s.at[i], e_r.at[i], at.peer(i)).wait_recv()
            total = rgr[0].astype(F32)
            for i in range(1, 16):
                total = total + rgr[i].astype(F32)
            total = total.astype(BF)
            for wl in wloads:
                wl.wait()
            rg[...] = (dot(total[:, :640], wts[0].reshape(1280, 640), 1, 1)
                       + dot(total[:, 640:], wts[1].reshape(1280, 640), 1, 1)).astype(BF)
    for copy in sends:
        copy.wait_send()


def reduce_all(dws, dwt, gr, full):
    dma = pltpu.SemaphoreType.DMA
    s = jax.ShapeDtypeStruct
    tall, flat = s((80, 640), F32), s((40, 1280), F32)
    v = pltpu.VMEM
    b = (80, 640)
    return pl.pallas_call(
        reduce_kernel,
        out_shape=(tall, tall, tall, flat) * 2 + (s((8, 1280), BF),),
        in_specs=[ANY, ANY, VM, ANY],
        out_specs=(VM,) * 9,
        scratch_shapes=[v((2, 2, 4, 4) + b, BF), v((2, 2, 4, 4) + b, BF), v((2, 2, 4) + b, BF), v((2, 2, 4) + b, BF),
                        v((2, 4) + b, BF), v((2, 2, 4) + b, BF), v((2, 4) + b, BF), v((2,) + b, BF),
                        v((2, 2) + b, BF), v((2, 4) + b, BF), v((2, 4) + b, BF), v((16, 8, 1280), BF),
                        v((2, 16) + b, BF)]
        + [dma((2, 2, 4))] * 3 + [dma((2, 2))] * 4 + [dma((2, 4))] * 2 + [dma((2, 2, 4))] * 2
        + [dma((2, 2))] * 4 + [dma((2, 3))] * 2 + [dma((2, 2))] * 4 + [dma((16,))] * 2 + [dma((2,))],
        compiler_params=pltpu.CompilerParams(collective_id=3, has_side_effects=True, vmem_limit_bytes=60 << 20),
        name="reduce_gradients",
    )(dws, dwt, gr, full)

def position_table(count, width):
    frame_ids = jnp.arange(count, dtype=jnp.int32).astype(F32)
    halves = jnp.arange(width // 2, dtype=jnp.int32).astype(F32)
    rates = jnp.exp(halves * (-2.0 * math.log(10000.0) / width))
    angles = frame_ids[:, None] * rates[None, :]
    return jnp.stack([jnp.sin(angles), jnp.cos(angles)], -1).reshape(count, width)


def per_device(frames_in, ref_feats, out_grad, space_query, space_key, space_value, space_output,
               time_query, time_key, time_value, time_output):
    def narrow(weight):
        return jnp.concatenate([weight[:, :640], weight[:, 640:]], 0)

    pack = jnp.stack([space_query, space_key, space_value, narrow(space_output),
                      time_query, time_key, time_value, narrow(time_output)])
    full, refs = gather(pack, jnp.pad(ref_feats[0], ((0, 2), (0, 0))))
    refs = refs.reshape(128, 1280)
    frames, grads = frames_in.reshape(192, 1280), out_grad.reshape(192, 1280)
    h1, qkv, rkv, o, h1r, ogr = space(frames, refs, grads, full)
    backr, dwt = temporal(h1r, ogr, position_table(32, 1280), full)
    out, frames_grad, dws, gr = back(backr, frames, refs, h1, qkv, rkv, o, full)
    *totals, rg = reduce_all(dws, dwt, gr.reshape(16, 8, 1280), full)
    return (out.reshape(frames_in.shape), frames_grad.reshape(frames_in.shape), rg[None, :6], *totals)


def solution(mesh):
    rows, refs, weight = P("clip", "frame", None, None), P("clip", "frame", None), P("frame", None)
    return jax.shard_map(
        per_device, mesh=mesh, in_specs=(rows, refs, rows) + (weight,) * 8,
        out_specs=(rows, rows, refs) + (weight,) * 8, check_vma=False)
```

time: 1260 us -> 255 us (0.20); the launches traced: 1250 us -> 254 us
  waiting for transfers between devices: 991 us -> 0 us
  Pallas kernels: 0 us -> 228 us
  matrix products: 81.4 us -> 0 us
  blocking collectives: 47.6 us -> 0 us
  starting transfers between devices: 36.3 us -> 0 us
  local copies, waits for them, and re-layouts: 51.1 us -> 24.9 us
  other arithmetic: 23.1 us -> 0.42 us
  between operations: 15.9 us -> 0.75 us
    reduce_scatter x8 -> x0, waiting for transfers between devices: 519 us -> none  [the longest x1 67 us: per_device(): lax.psum_scatter(term_sv.astype(jnp.bfloat16), 'frame', scatter_dimension...]
    pallas_call x0 -> x5, Pallas kernels: none -> 228 us  [the longest x1 98.1 us: reduce_all(): pl.pallas_call(reduce_kernel, out_shape=(tall, tall, tall, flat) * 2 + (s...]
    all_gather x8 -> x0, waiting for transfers between devices: 223 us -> none  [the longest x1 35.2 us: per_device(): lax.all_gather(space_value, 'frame', axis=0, tiled=True)]
    psum x1 -> x0, waiting for transfers between devices: 168 us -> none  [per_device(): lax.psum(share_sq.astype(jnp.bfloat16), 'clip').astype(jnp.float32)]
    dot_general x42 -> x0, matrix products: 81.4 us -> none  [the longest x12 28.3 us: product(): return jnp.einsum(form, left, right, preferred_element_type=jnp.float32)]
    unnamed x19 -> x0, waiting for transfers between devices: 79.4 us -> none
    all_to_all x7 -> x0, starting transfers between devices: 35.2 us -> none  [the longest x1 5.71 us: per_device(): lax.all_to_all(merge_heads(token_key_grad).astype(jnp.bfloat16), 'frame',...]
    all_gather x2 -> x0, blocking collectives: 34.5 us -> none  [the longest x1 17.3 us: per_device(): lax.all_gather(own_key, 'frame', axis=0, tiled=True)]
  transfers between devices with their start and end apart: 25 -> 0, of which waited for: 20 -> 0; matrix products, arithmetic and copies ran while one was open for 9% -> 0% of each run, Pallas kernels for 0% -> 0%
where the time goes in v1:
time: 255 us; the launch traced here: 254 us
  Pallas kernels  228 us (89%)
  local copies, waits for them, and re-layouts  24.9 us (10%)
    pallas_call x1, Pallas kernels, reduce_all(): pl.pallas_call(reduce_kernel, out_shape=(tall, tall, tall, flat) * 2 + (s...  98.1 us
    pallas_call x1, Pallas kernels, gather(): pl.pallas_call(gather_kernel, out_shape=(jax.ShapeDtypeStruct((16, 8, 80,...  63.3 us
    pallas_call x1, Pallas kernels, temporal(): pl.pallas_call(time_kernel, out_shape=(s((256, 1920), BF), s((2, 2, 4, 4,...  27.5 us
    pallas_call x1, Pallas kernels, space(): pl.pallas_call(space_kernel, out_shape=(s((192, 1280), BF), s((3, 192, 64...  23.8 us
    unnamed x16, local copies, waits for them, and re-layouts  19.3 us
    pallas_call x1, Pallas kernels, back(): pl.pallas_call(back_kernel, out_shape=(s((192, 1280), BF), s((192, 1280),...  15.3 us

profile of v1, /device:TPU:32, one launch (start us, length us, event | category | flops | bytes accessed | tf_op | source)
XLA Modules:
  0.0 254.1 jit_solution(4908895459127698053)
XLA Ops:
  0.7 1.3 pad.4.ref8
  2.0 0.8 fusion.3
  2.8 0.8 fusion.2
  3.7 0.4 multiply_sine_fusion
  4.1 0.3 copy.23
  4.4 0.9 copy.24.table
  5.2 0.9 bitcast_dynamic-update-slice_fusion.5
  6.2 0.9 bitcast_dynamic-update-slice_fusion.4
  7.1 0.9 bitcast_dynamic-update-slice_fusion.3
  8.0 0.9 bitcast_dynamic-update-slice_fusion.2
  8.9 0.9 bitcast_dynamic-update-slice_fusion.1
  9.8 0.9 bitcast_dynamic-update-slice_fusion
  10.8 0.0 copy-start
  10.8 0.9 copy-done
  11.7 63.3 %gather_weights.1 = (bf16[16,8,80,640]{3,2,1,0:T(8,128)(2,1)}, bf16[16,8,1280]{2,1,0:T(8,128)(2,1)}) custom-call(bf16[8,80,640]{2,1,0:T(8,128)(2,1)} %copy-done, bf16[8,1280]{1,0:T(8,128)(2,1)} %pad.4.ref8), custom_call_target="tpu_custom_call" | custom-call | tf_op jit(solution)/shard_map/gather_weights/pallas_call | solution.py:182
  75.0 23.8 %space_forward.1 = (bf16[192,1280]{1,0:T(8,128)(2,1)}, bf16[3,192,640]{2,1,0:T(8,128)(2,1)}, bf16[2,96,640]{2,1,0:T(8,128)(2,1)}, bf16[192,640]{1,0:T(8,128)(2,1...) custom-call(bf16[192,1280]{1,0:T(8,128)(2,1)} %bitcast.31, bf16[128,1280]{1,0:T(8,128)(2,1)} %bitcast.33, ...), custom_call_target="tpu_custom_call" | custom-call | tf_op jit(solution)/shard_map/space_forward/pallas_call | solution.py:367
  98.8 27.5 %time_both.1 = (bf16[256,1920]{1,0:T(8,128)(2,1)}, bf16[2,2,4,4,80,640]{5,4,3,2,1,0:T(8,128)(2,1)}) custom-call(bf16[256,1280]{1,0:T(8,128)(2,1)} %get-tuple-element.36.h1r, bf16[256,1280]{1,0:T(8,128)(2,1)} %get-tuple-element.37.ogr, f32[32,1280]{1,0:T(8,128)} %copy.24.table, bf16[16,8,80,640]{3,2,1,0:T(8,128)(2,1)} %get-tuple-element.35.full), custom_call_target="tpu_custom_call" | custom-call | tf_op jit(solution)/shard_map/time_both/pallas_call | solution.py:430
  126.3 15.3 %space_backward.1 = (bf16[192,1280]{1,0:T(8,128)(2,1)}, bf16[192,1280]{1,0:T(8,128)(2,1)}, bf16[2,2,4,4,80,640]{5,4,3,2,1,0:T(8,128)(2,1)}, bf16[128,1280]{1,0:T(8,128)(2,1)}) custom-call(bf16[256,1920]{1,0:T(8,128)(2,1)} %get-tuple-element.38.backr, bf16[192,1280]{1,0:T(8,128)(2,1)} %bitcast.32, bf16[128,1280]{1,0:T(8,128)(2,1)} %bitcast.34, ...), custom_call_target="tpu_custom_call" | custom-call | tf_op jit(solution)/shard_map/space_backward/pallas_call | solution.py:497
  141.6 98.1 %reduce_gradients.1 = (f32[80,640]{1,0:T(8,128)}, f32[80,640]{1,0:T(8,128)}, f32[80,640]{1,0:T(8,128)}, f32[40,1280]{1,0:T(8,128)}, f32[80,640]{1,0:T(8,128)}, /...) custom-call(bf16[2,2,4,4,80,640]{5,4,3,2,1,0:T(8,128)(2,1)} %get-tuple-element.45.dws, ...), custom_call_target="tpu_custom_call" | custom-call | tf_op jit(solution)/shard_map/reduce_gradients/pallas_call | solution.py:666
  239.8 1.3 slice_bitcast_fusion
  241.1 1.6 copy.40
  242.8 1.6 copy.41
  244.4 1.6 copy.42
  246.0 1.6 copy.43
  247.6 1.6 copy.44
  249.2 1.6 copy.45
  250.9 1.6 copy.46
  252.5 1.6 copy.47
  (5 shorter events, 0.1 us)
Async XLA Ops:
  10.8 0.9 copy-start

commit v2 on v1

v2 whole, which is shorter than its diff:
```python
import math

import jax
import jax.numpy as jnp
from jax import lax
from jax.experimental import pallas as pl
from jax.experimental.pallas import tpu as pltpu
from jax.sharding import PartitionSpec as P


MESH = pl.DeviceIdType.MESH
ANY = pl.BlockSpec(memory_space=pl.ANY)
VM = pl.BlockSpec(memory_space=pltpu.VMEM)


class Place:
    def __init__(self):
        clip, frame = lax.axis_index("clip"), lax.axis_index("frame")
        self.clip, self.frame = clip, frame
        self.x, self.zh = lax.rem(clip, 4), lax.div(clip, 4)
        self.y, self.zl, self.core = lax.div(frame, 4), lax.rem(lax.div(frame, 2), 2), lax.rem(frame, 2)
        self.parity = lax.rem(self.x, 2)
        self.sibling = (clip, frame + 1 - 2 * self.core)

    def along_y(self, step):
        return (self.clip, lax.rem(self.y + 4 + step, 4) * 4 + self.zl * 2 + self.core)

    def along_x(self, step):
        return (self.zh * 4 + lax.rem(self.x + 4 + step, 4), self.frame)

    def along_z(self, step):
        far = lax.rem(self.zh * 2 + self.zl + 8 + step, 8)
        return (lax.div(far, 2) * 4 + self.x, self.y * 4 + lax.rem(far, 2) * 2 + self.core)

    def along_zh(self, step):
        return (lax.rem(self.zh + 4 + step, 4) * 4 + self.x, self.frame)

    def peer(self, step):
        return (self.clip, lax.rem(self.frame + step, 16))


def greet(devices):
    barrier = pltpu.get_barrier_semaphore()
    for device in devices:
        pl.semaphore_signal(barrier, inc=1, device_id=device, device_id_type=MESH)
    pl.semaphore_wait(barrier, len(devices))


def remote(src, dst, send, recv, device):
    return pltpu.make_async_remote_copy(
        src_ref=src, dst_ref=dst, send_sem=send, recv_sem=recv, device_id=device, device_id_type=MESH)


def shard_of(y, zl, core):
    return lax.rem(y + 8, 4) * 4 + zl * 2 + core


BF, F32 = jnp.bfloat16, jnp.float32
EPSILON = 1e-05
SCALE = 160 ** -0.5


def dot(a, b, ca=1, cb=0):
    return lax.dot_general(a, b, (((ca,), (cb,)), ((), ())), preferred_element_type=F32)


def stats(wide):
    offset = wide - jnp.mean(wide, -1, keepdims=True)
    inverse = lax.rsqrt(jnp.mean(offset * offset, -1, keepdims=True) + EPSILON)
    return offset * inverse, inverse


def stats_back(centred, inverse, g):
    first = jnp.mean(g, -1, keepdims=True)
    second = jnp.mean(g * centred, -1, keepdims=True)
    return inverse * (g - first - centred * second)


def iota(shape, dim):
    return lax.broadcasted_iota(jnp.int32, shape, dim)


def one_hot(hit):
    return jnp.where(hit, 1.0, 0.0).astype(BF)


def frame_pack():
    r, c = iota((256, 192), 0), iota((256, 192), 1)
    d, j = lax.shift_right_logical(r, 4), lax.bitwise_and(r, 15)
    a = jnp.where(j >= 6, 1, 0)
    return one_hot((j < 12) & (c == 90 * a + 6 * d + j))


def frame_unpack():
    c, r = iota((192, 256), 0), iota((192, 256), 1)
    d, j = lax.shift_right_logical(r, 4), lax.bitwise_and(r, 15)
    a = jnp.where(j >= 6, 1, 0)
    return one_hot((j < 12) & (c == 90 * a + 6 * d + j))


def token_unpack():
    m, r = iota((192, 256), 0), iota((192, 256), 1)
    t, f, a = lax.shift_right_logical(m, 5), lax.bitwise_and(lax.shift_right_logical(m, 1), 15), lax.bitwise_and(m, 1)
    return one_hot(r == 16 * f + 6 * a + t)


def token_pack():
    m, r = iota((256, 192), 1), iota((256, 192), 0)
    t, f, a = lax.shift_right_logical(m, 5), lax.bitwise_and(lax.shift_right_logical(m, 1), 15), lax.bitwise_and(m, 1)
    return one_hot(r == 16 * f + 6 * a + t)


def ref_unpack(rows, cols, swap=False):
    m, r = (iota((rows, cols), 0), iota((rows, cols), 1)) if not swap else (iota((rows, cols), 1), iota((rows, cols), 0))
    d, j = lax.shift_right_logical(r, 3), lax.bitwise_and(r, 7)
    return one_hot((j < 6) & (m == 6 * d + j))


def head_masks():
    lane = iota((1, 640), 1)
    return [(lane >= 160 * h) & (lane < 160 * (h + 1)) for h in range(4)]


def stack_heads(rows, masks):
    return jnp.concatenate([rows * one_hot(m) for m in masks], 0)


def merge_heads(stacked, masks):
    n = stacked.shape[0] // 4
    total = jnp.where(masks[0], stacked[:n], 0.0)
    for h in range(1, 4):
        total = jnp.where(masks[h], stacked[h * n:(h + 1) * n], total)
    return total


def softmax(stacked, keys, same=None):
    powers = jnp.exp(dot(stacked, keys, 1, 1) * SCALE)
    if same is not None:
        powers = jnp.where(same, powers, 0.0)
    return powers / jnp.sum(powers, -1, keepdims=True)


def score_back(probs, grads, values):
    dp = dot(grads, values, 1, 1)
    return (probs * (dp - jnp.sum(probs * dp, -1, keepdims=True)) * SCALE).astype(BF)


def wide_output(slot):
    wide = slot.astype(F32)
    left = wide[:, :40].reshape(640, 640).astype(BF)
    right = wide[:, 40:].reshape(640, 640).astype(BF)
    return left, right


def pack_output(left, right):
    return jnp.concatenate([left.reshape(16, 40, 640), right.reshape(16, 40, 640)], 1)


def store_term(dw, w, term):
    parts = term.reshape(4, 2, 2, 80, 640).astype(BF)
    for core in range(2):
        for zl in range(2):
            dw[core, zl, w] = parts[:, zl, core]


def exchange_start(at, src, dst, send, recv):
    copies = []
    for i in range(1, 16):
        to = lax.rem(at.frame + i, 16)
        copy = remote(src.at[pl.ds(pl.multiple_of(16 * to, 16), 16)],
                      dst.at[pl.ds(pl.multiple_of(16 * at.frame, 16), 16)], send.at[i], recv.at[i], at.peer(i))
        copy.start()
        copies.append(copy)
    own = pl.ds(pl.multiple_of(16 * at.frame, 16), 16)
    dst[own, :] = src[own, :]
    return copies


def load(src, dst, sem):
    copy = pltpu.make_async_copy(src, dst, sem)
    copy.start()
    return copy


def time_kernel(h1r, ogr, table, full, back, dw, wts, buf, wsem, s_s, r_s):
    at = Place()
    loads = [load(full.at[:, i], wts.at[i], wsem.at[i]) for i in range(4)]
    greet([at.peer(i) for i in range(1, 16)])
    masks = head_masks()
    unpack = token_unpack()
    h1 = dot(unpack, h1r[...])
    og = dot(unpack, ogr[...]).astype(BF)
    centred, inverse = stats(h1)
    n2 = (centred + jnp.concatenate([table[...]] * 6, 0)).astype(BF)
    parts = []
    for i in range(3):
        loads[i].wait()
        parts.append(dot(n2, wts[i].reshape(1280, 640)).astype(BF))
    q, k, v = parts
    r, c = iota((768, 192), 0), iota((768, 192), 1)
    r = jnp.where(r >= 384, r - 384, r)
    r = jnp.where(r >= 192, r - 192, r)
    same = lax.shift_right_logical(r, 5) == lax.shift_right_logical(c, 5)
    qs = stack_heads(q, masks)
    probs = softmax(qs, k, same)
    pb = probs.astype(BF)
    o2 = merge_heads(dot(pb, v), masks).astype(BF)
    loads[3].wait()
    left, right = wide_output(wts[3])
    go = (dot(og[:, :640], left, 1, 1) + dot(og[:, 640:], right, 1, 1)).astype(BF)
    gs = stack_heads(go, masks)
    eb = score_back(probs, gs, v)
    gq = merge_heads(dot(eb, k), masks).astype(BF)
    gk = dot(eb, qs, 0, 0).astype(BF)
    gv = dot(pb, gs, 0, 0).astype(BF)
    grads = (gq, gk, gv)
    gn = dot(gq, wts[0].reshape(1280, 640), 1, 1)
    for i in (1, 2):
        gn = gn + dot(grads[i], wts[i].reshape(1280, 640), 1, 1)
    gh = (og.astype(F32) + stats_back(centred, inverse, gn)).astype(BF)
    pack = token_pack()
    buf[:, :1280] = dot(pack, gh).astype(BF)
    buf[:, 1280:] = dot(pack, o2).astype(BF)
    copies = exchange_start(at, buf, back, s_s, r_s)
    for i in range(3):
        store_term(dw, i, dot(n2, grads[i], 0, 0))
    store_term(dw, 3, pack_output(dot(o2, og[:, :640], 0, 0), dot(o2, og[:, 640:], 0, 0)))
    for copy in copies:
        copy.wait()


def temporal(h1r, ogr, table, full):
    dma = pltpu.SemaphoreType.DMA
    s = jax.ShapeDtypeStruct
    return pl.pallas_call(
        time_kernel,
        out_shape=(s((256, 1920), BF), s((2, 2, 4, 4, 80, 640), BF)),
        in_specs=[VM, VM, VM, ANY],
        out_specs=(VM, VM),
        scratch_shapes=[pltpu.VMEM((4, 16, 80, 640), BF), pltpu.VMEM((256, 1920), BF),
                        dma((4,)), dma((16,)), dma((16,))],
        compiler_params=pltpu.CompilerParams(collective_id=2, has_side_effects=True, vmem_limit_bytes=60 << 20),
        name="time_both",
    )(h1r, ogr, table, full)


def first_kernel(frames, ref_in, og, w0, w1, w2, w3, w4, w5, w6, w7,
                 h1_o, qkv_o, rkv_o, o_o, h1r, ogr, refs, full_so, full_t,
                 pack, ref8, full_s, buf_a, buf_b, sib_s, sib_r, y_s, y_r, rel_s, rel_r, z_s, z_r, x_s, x_r,
                 ref_s, ref_r, s_s, r_s, loc):
    at = Place()
    y, zl, core, p, me = at.y, at.zl, at.core, at.parity, at.frame
    for i, w in enumerate((w0, w1, w2, None, w4, w5, w6)):
        if w is not None:
            pack[i] = w[...]
    for i, w in ((3, w3), (7, w7)):
        wide = w[...].astype(F32)
        pack[i] = jnp.concatenate([wide[:, :640], wide[:, 640:]], 0).astype(BF)
    small = ref_in[...].astype(F32)
    ref8[...] = jnp.concatenate([small, small[:2] * 0.0], 0).astype(BF)
    greet([at.along_x(1), at.along_x(-1), at.along_z(1), at.along_z(-1)] + [at.peer(i) for i in range(1, 16)])
    sends = []

    def go(copy):
        copy.start()
        sends.append(copy)

    steps = (1, -1)
    fulls = (full_s, full_t)
    keeps = []

    def chain(h):
        full = fulls[h]
        rows = [shard_of(y + k, zl, core) for k in range(4)]
        over = [shard_of(y + k, 1 - zl, core) for k in range(4)]

        def pair(j):
            return pl.ds(2 * j, 2)

        def to_sibling(index, ref):
            go(remote(ref, ref, sib_s.at[h, index], sib_r.at[h, index], at.sibling))

        def z_send(k, src=None):
            for d in range(2):
                w = 2 * p + d
                dst = full.at[rows[k], w]
                go(remote(dst if src is None else src.at[4 * h + w], dst, z_s.at[h, k, d], z_r.at[h, k, d],
                          at.along_z(1 - 2 * d)))

        def z_wait(k):
            for d in range(2):
                ref = full.at[over[k], 2 * p + d]
                remote(ref, ref, z_s.at[h, k, d], z_r.at[h, k, d], at.along_z(1)).wait_recv()
                go(remote(ref, ref, x_s.at[h, k, d], x_r.at[h, k, d], at.along_x(1 - 2 * d)))
                to_sibling(7 + 2 * k + d, ref)

        def x_wait(k):
            for d in range(2):
                ref = full.at[over[k], 2 * (1 - p) + d]
                remote(ref, ref, x_s.at[h, k, d], x_r.at[h, k, d], at.along_x(1)).wait_recv()
                to_sibling(15 + 2 * k + d, ref)

        half = pl.ds(4 * h, 4)
        for j in range(2):
            for s, step in enumerate(steps):
                go(remote(pack.at[pl.ds(4 * h + 2 * j, 2)], full.at[me, pair(j)], y_s.at[h, s, j], y_r.at[h, s, j],
                          at.along_y(step)))
        z_send(0, pack)
        go(remote(pack.at[half], full.at[me], sib_s.at[h, 0], sib_r.at[h, 0], at.sibling))
        keeps.append(load(pack.at[half], full.at[me], loc.at[h]))
        yield
        for j in range(2):
            for s, step in enumerate(steps):
                ref = full.at[rows[(4 - step) % 4], pair(j)]
                remote(ref, ref, y_s.at[h, s, j], y_r.at[h, s, j], at.along_y(step)).wait_recv()
                if j == s:
                    go(remote(ref, ref, rel_s.at[h, j], rel_r.at[h, j], at.along_y(step)))
                to_sibling(1 + 2 * s + j, ref)
        z_send(1)
        z_send(3)
        yield
        z_wait(0)
        for j in range(2):
            ref = full.at[rows[2], pair(j)]
            remote(ref, ref, rel_s.at[h, j], rel_r.at[h, j], at.along_y(1)).wait_recv()
            to_sibling(5 + j, ref)
        z_send(2)
        yield
        z_wait(1)
        z_wait(3)
        x_wait(0)
        yield
        z_wait(2)
        x_wait(1)
        x_wait(3)
        yield
        x_wait(2)
        yield

        def sib_wait(index, ref):
            remote(ref, ref, sib_s.at[h, index], sib_r.at[h, index], at.sibling).wait_recv()

        other = [shard_of(y + k, zl, 1 - core) for k in range(4)]
        sib_wait(0, full.at[other[0]])
        for s, step in enumerate(steps):
            for j in range(2):
                sib_wait(1 + 2 * s + j, full.at[other[(4 - step) % 4], pair(j)])
        for j in range(2):
            sib_wait(5 + j, full.at[other[2], pair(j)])
        for k in range(4):
            for d in range(2):
                far = shard_of(y + k, 1 - zl, 1 - core)
                sib_wait(7 + 2 * k + d, full.at[far, 2 * p + d])
                sib_wait(15 + 2 * k + d, full.at[far, 2 * (1 - p) + d])

    now, later = chain(0), chain(1)
    next(now)
    for i in range(1, 16):
        go(remote(ref8, refs.at[me], ref_s.at[i], ref_r.at[i], at.peer(i)))
    refs[me] = ref8[...]
    pack_rows = frame_pack()
    buf_a[...] = dot(pack_rows, og[...]).astype(BF)
    masks = head_masks()
    wide = frames[...].astype(F32)
    n1 = stats(wide)[0].astype(BF)
    next(now)
    next(now)
    next(later)
    next(now)
    next(now)
    next(now)
    for i in range(1, 16):
        ref = refs.at[lax.rem(me + 16 - i, 16)]
        remote(ref, ref, ref_s.at[i], ref_r.at[i], at.peer(i)).wait_recv()
    for _ in now:
        pass
    keeps[0].wait()
    keep = load(full_s, full_so, loc.at[2])
    copies = exchange_start(at, buf_a, ogr, s_s.at[0], r_s.at[0])
    ref = dot(ref_unpack(96, 128), refs[...].astype(F32).reshape(128, 1280).astype(BF)).astype(BF)
    q = dot(n1, full_s[:, 0].reshape(1280, 640)).astype(BF)
    w = full_s[:, 1].reshape(1280, 640)
    k, rk = dot(n1, w).astype(BF), dot(ref, w).astype(BF)
    next(later)
    w = full_s[:, 2].reshape(1280, 640)
    v, rv = dot(n1, w).astype(BF), dot(ref, w).astype(BF)
    for i, part in enumerate((q, k, v)):
        qkv_o[i] = part
    rkv_o[0] = rk
    rkv_o[1] = rv
    outs = []
    for a in range(2):
        rows = slice(96 * a, 96 * a + 96)
        keys = jnp.concatenate([k[rows], rk], 0)
        values = jnp.concatenate([v[rows], rv], 0)
        probs = softmax(stack_heads(q[rows], masks), keys).astype(BF)
        outs.append(merge_heads(dot(probs, values), masks))
        next(later)
    o = jnp.concatenate(outs, 0).astype(BF)
    o_o[...] = o
    left, right = wide_output(full_s[:, 3])
    h1 = (wide + jnp.concatenate([dot(o, left), dot(o, right)], 1)).astype(BF)
    h1_o[...] = h1
    buf_b[...] = dot(pack_rows, h1).astype(BF)
    copies += exchange_start(at, buf_b, h1r, s_s.at[1], r_s.at[1])
    for _ in later:
        pass
    for copy in copies:
        copy.wait()
    for copy in sends:
        copy.wait_send()
    keep.wait()
    keeps[1].wait()


def first(frames, ref_in, og, weights):
    dma = pltpu.SemaphoreType.DMA
    s = jax.ShapeDtypeStruct
    v = pltpu.VMEM
    return pl.pallas_call(
        first_kernel,
        out_shape=(s((192, 1280), BF), s((3, 192, 640), BF), s((2, 96, 640), BF), s((192, 640), BF),
                   s((256, 1280), BF), s((256, 1280), BF), s((16, 8, 1280), BF), s((16, 4, 80, 640), BF),
                   s((16, 4, 80, 640), BF)),
        in_specs=[VM] * 11,
        out_specs=(VM,) * 7 + (ANY, ANY),
        scratch_shapes=[v((8, 80, 640), BF), v((8, 1280), BF), v((16, 4, 80, 640), BF), v((256, 1280), BF),
                        v((256, 1280), BF), dma((2, 23)), dma((2, 23)), dma((2, 2, 2)), dma((2, 2, 2)), dma((2, 2)),
                        dma((2, 2)), dma((2, 4, 2)), dma((2, 4, 2)), dma((2, 4, 2)), dma((2, 4, 2)), dma((16,)),
                        dma((16,)), dma((2, 16)), dma((2, 16)), dma((3,))],
        compiler_params=pltpu.CompilerParams(collective_id=0, has_side_effects=True, vmem_limit_bytes=60 << 20),
        name="gather_and_space_forward",
    )(frames, ref_in, og, *weights)


def add(*parts):
    total = parts[0].astype(F32)
    for part in parts[1:]:
        total = total + part.astype(F32)
    return total


def last_kernel(backr, frames, refs, h1, qkv, rkv, o_in, full_s, full_t, dwt,
                out_o, fg_o, rg, fin,
                wts, dws, gt, r0, rx, rz, ry1, ry2, pm, rax1, rax2, rq, gr, rgr,
                wsem, l_m, c_s, c_r, x_s, x_r, z_s, z_r, y1_s, y1_r, y2_s, y2_r,
                a1_s, a1_r, a2_s, a2_r, q_s, q_r, qq_s, qq_r, g_s, g_r, gg_s, gg_r, e_s, e_r):
    at = Place()
    y, zl, p, x, zh, me = at.y, at.zl, at.parity, at.x, at.zh, at.frame
    core, oz = at.core, 1 - at.zl
    loads = {7: load(full_t.at[:, 3], wts.at[0], wsem.at[0])}
    for n, i in enumerate((3, 0, 1, 2)):
        loads[i] = load(full_s.at[:, i], wts.at[1 + n], wsem.at[1 + n])
    mine = {}
    for a, zz in enumerate((oz, zl)):
        for w in range(4):
            mine[a, w] = load(dwt.at[core, zz, w], gt.at[zz, w], l_m.at[a, w])
    greet([at.peer(i) for i in range(1, 16)] + [at.along_x(1), at.along_x(-1), at.along_z(1), at.along_z(-1),
                                                at.along_zh(1), at.along_zh(-1)])
    sends = []

    def go(copy):
        copy.start()
        sends.append(copy)
        return copy

    def rem4(v):
        return lax.rem(v + 8, 4)

    cross = {}

    def send_cross(h, w):
        src = dws if h == 0 else dwt
        for a, zz in enumerate((oz, zl)):
            cross[h, a, w] = go(remote(src.at[1 - core, zz, w], r0.at[h, a, w], c_s.at[h, a, w], c_r.at[h, a, w],
                                       at.sibling))

    def chain(h):
        g = dws.at[core] if h == 0 else gt
        low, high = pl.ds(0, 48), pl.ds(48, 32)
        ys = [rem4(y + k) for k in range(4)]
        xc, zc = {}, {}

        def take(a, zz):
            for w in range(4):
                if h == 1:
                    mine[a, w].wait()
                cross[h, a, w].wait_recv()
                g[zz, w] = add(g[zz, w], r0[h, a, w]).astype(BF)

        def x_take(k):
            for d in range(2):
                xc[k, d].wait_recv()
                w = 2 * p + d
                g[oz, w, ys[k]] = add(g[oz, w, ys[k]], rx[h, d, k]).astype(BF)
                zc[k, d] = go(remote(g.at[oz, w, ys[k]], rz.at[h, d, k], z_s.at[h, d, k], z_r.at[h, d, k],
                                     at.along_z(2 * d - 1)))

        def z_take(k):
            for d in range(2):
                zc[k, d].wait_recv()
                w = 2 * p + d
                g[zl, w, ys[k]] = add(g[zl, w, ys[k]], rz[h, d, k]).astype(BF)

        take(0, oz)
        for k in (2, 1, 3, 0):
            for d in range(2):
                xc[k, d] = go(remote(g.at[oz, 2 * (1 - p) + d, ys[k]], rx.at[h, d, k], x_s.at[h, d, k],
                                     x_r.at[h, d, k], at.along_x(2 * d - 1)))
        take(1, zl)
        yield
        x_take(2)
        x_take(1)
        yield
        z_take(2)
        y1 = [go(remote(g.at[zl, w, ys[2]], ry1.at[h, w], y1_s.at[h, w], y1_r.at[h, w],
                        at.along_y(-1 if w < 2 else 1))) for w in range(4)]
        x_take(3)
        yield
        x_take(0)
        z_take(1)
        z_take(3)
        yield
        y2 = {}
        for w in (0, 2, 1, 3):
            y1[w].wait_recv()
            on = ys[3 if w < 2 else 1]
            g[zl, w, on] = add(g[zl, w, on], ry1[h, w]).astype(BF)
            for s, step in enumerate((1, -1)):
                y2[s, w] = go(remote(g.at[zl, w, ys[step % 4]], ry2.at[s, h, w], y2_s.at[s, h, w],
                                     y2_r.at[s, h, w], at.along_y(step)))
        z_take(0)
        yield
        for w in (0, 2, 1, 3):
            y2[0, w].wait_recv()
            y2[1, w].wait_recv()
            pm[h, w] = add(g[zl, w, y], ry2[0, h, w], ry2[1, h, w]).astype(BF)
        far = rem4(x + 2)
        a1 = [go(remote(pm.at[h, far, part], rax1.at[h, part], a1_s.at[h, s], a1_r.at[h, s], at.along_x(step)))
              for s, (step, part) in enumerate(((1, low), (-1, high)))]
        yield
        for s, (step, part) in enumerate(((1, low), (-1, high))):
            a1[s].wait_recv()
            on = rem4(x + step)
            pm[h, on, part] = add(pm[h, on, part], rax1[h, part]).astype(BF)
        a2 = [go(remote(pm.at[h, rem4(x + step)], rax2.at[s, h], a2_s.at[s, h], a2_r.at[s, h], at.along_x(step)))
              for s, step in enumerate((1, -1))]
        yield
        for copy in a2:
            copy.wait_recv()
        rq[h, zh] = add(pm[h, x], rax2[0, h], rax2[1, h]).astype(BF)
        for s, step in enumerate((1, -1)):
            go(remote(rq.at[h, zh], rq.at[h, zh], q_s.at[h, s], q_r.at[h, s], at.along_zh(step)))
        yield
        for s, (step, part) in enumerate(((1, low), (-1, high))):
            ref = rq.at[h, rem4(zh - step)]
            remote(ref, ref, q_s.at[h, s], q_r.at[h, s], at.along_zh(step)).wait_recv()
            ref = rq.at[h, rem4(zh - step), part]
            go(remote(ref, ref, qq_s.at[h, s], qq_r.at[h, s], at.along_zh(step)))
        yield
        for s, (step, part) in enumerate(((1, low), (-1, high))):
            ref = rq.at[h, rem4(zh + 2), part]
            remote(ref, ref, qq_s.at[h, s], qq_r.at[h, s], at.along_zh(step)).wait_recv()
        fin[h, x] = add(rq[h, 0], rq[h, 1], rq[h, 2], rq[h, 3]).astype(BF)
        for s, step in enumerate((1, -1)):
            go(remote(fin.at[h, x], fin.at[h, x], g_s.at[h, s], g_r.at[h, s], at.along_x(step)))
        yield
        for s, (step, part) in enumerate(((1, low), (-1, high))):
            ref = fin.at[h, rem4(x - step)]
            remote(ref, ref, g_s.at[h, s], g_r.at[h, s], at.along_x(step)).wait_recv()
            ref = fin.at[h, rem4(x - step), part]
            go(remote(ref, ref, gg_s.at[h, s], gg_r.at[h, s], at.along_x(step)))
        yield
        for s, (step, part) in enumerate(((1, low), (-1, high))):
            ref = fin.at[h, rem4(x + 2), part]
            remote(ref, ref, gg_s.at[h, s], gg_r.at[h, s], at.along_x(step)).wait_recv()

    for w in range(4):
        send_cross(1, w)
    early = chain(1)
    masks = head_masks()
    unpack = frame_unpack()
    gh = dot(unpack, backr[:, :1280]).astype(BF)
    o2 = dot(unpack, backr[:, 1280:]).astype(BF)
    next(early)
    loads[3].wait()
    left, right = wide_output(wts[1])
    go_ = (dot(gh[:, :640], left, 1, 1) + dot(gh[:, 640:], right, 1, 1)).astype(BF)
    rk, rv = rkv[0], rkv[1]
    gq, gk, gv = [], [], []
    grk = grv = None
    for a in range(2):
        rows = slice(96 * a, 96 * a + 96)
        keys = jnp.concatenate([qkv[1, rows], rk], 0)
        values = jnp.concatenate([qkv[2, rows], rv], 0)
        qs = stack_heads(qkv[0, rows], masks)
        gs = stack_heads(go_[rows], masks)
        probs = softmax(qs, keys)
        eb = score_back(probs, gs, values)
        gq.append(merge_heads(dot(eb, keys), masks))
        gkeys = dot(eb, qs, 0, 0)
        gvalues = dot(probs.astype(BF), gs, 0, 0)
        gk.append(gkeys[:96])
        gv.append(gvalues[:96])
        grk = gkeys[96:] if grk is None else grk + gkeys[96:]
        grv = gvalues[96:] if grv is None else grv + gvalues[96:]
        next(early)
    gq, gk, gv = (jnp.concatenate(g, 0).astype(BF) for g in (gq, gk, gv))
    grk, grv = grk.astype(BF), grv.astype(BF)
    centred, inverse = stats(frames[...].astype(F32))
    n1 = centred.astype(BF)
    ref = dot(ref_unpack(96, 128), refs[...]).astype(BF)
    o = o_in[...]
    store_term(dws, 3, pack_output(dot(o, gh[:, :640], 0, 0), dot(o, gh[:, 640:], 0, 0)))
    send_cross(0, 3)
    store_term(dws, 0, dot(n1, gq, 0, 0))
    send_cross(0, 0)
    store_term(dws, 1, dot(n1, gk, 0, 0) + dot(ref, grk, 0, 0))
    send_cross(0, 1)
    store_term(dws, 2, dot(n1, gv, 0, 0) + dot(ref, grv, 0, 0))
    send_cross(0, 2)
    spread = ref_unpack(128, 96, True)
    gr[:, :, :640] = dot(spread, grk).reshape(16, 8, 640).astype(BF)
    gr[:, :, 640:] = dot(spread, grv).reshape(16, 8, 640).astype(BF)
    rgr[me] = gr[me]
    late = chain(0)
    next(early)
    next(late)
    for i in range(1, 16):
        to = lax.rem(me + i, 16)
        go(remote(gr.at[to], rgr.at[me], e_s.at[i], e_r.at[i], at.peer(i)))

    def finish_rows():
        gn = None
        for n, (i, g) in enumerate(((0, gq), (1, gk), (2, gv))):
            loads[i].wait()
            term = dot(g, wts[2 + n].reshape(1280, 640), 1, 1)
            gn = term if gn is None else gn + term
        fg_o[...] = (gh.astype(F32) + stats_back(centred, inverse, gn)).astype(BF)

    def finish_out():
        loads[7].wait()
        left, right = wide_output(wts[0])
        out_o[...] = (h1[...].astype(F32) + jnp.concatenate([dot(o2, left), dot(o2, right)], 1)).astype(BF)

    def finish_ref():
        for i in range(1, 16):
            ref = rgr.at[lax.rem(me + 16 - i, 16)]
            remote(ref, ref, e_s.at[i], e_r.at[i], at.peer(i)).wait_recv()
        total = rgr[0].astype(F32)
        for i in range(1, 16):
            total = total + rgr[i].astype(F32)
        total = total.astype(BF)
        rg[...] = (dot(total[:, :640], wts[3].reshape(1280, 640), 1, 1)
                   + dot(total[:, 640:], wts[4].reshape(1280, 640), 1, 1)).astype(BF)

    work = [finish_rows, finish_out, finish_ref]
    live = [early, late]
    while live:
        if work:
            work.pop(0)()
        for c in list(live):
            try:
                next(c)
            except StopIteration:
                live.remove(c)
    for copy in sends:
        copy.wait_send()


def last(backr, frames, refs, h1, qkv, rkv, o, full_s, full_t, dwt):
    dma = pltpu.SemaphoreType.DMA
    s = jax.ShapeDtypeStruct
    v = pltpu.VMEM
    b = (80, 640)
    return pl.pallas_call(
        last_kernel,
        out_shape=(s((192, 1280), BF), s((192, 1280), BF), s((8, 1280), BF), s((2, 4) + b, BF)),
        in_specs=[VM] * 7 + [ANY] * 3,
        out_specs=(VM,) * 4,
        scratch_shapes=[v((5, 16) + b, BF), v((2, 2, 4, 4) + b, BF), v((2, 4, 4) + b, BF), v((2, 2, 4, 4) + b, BF),
                        v((2, 2, 4) + b, BF), v((2, 2, 4) + b, BF), v((2, 4) + b, BF), v((2, 2, 4) + b, BF),
                        v((2, 4) + b, BF), v((2,) + b, BF), v((2, 2) + b, BF), v((2, 4) + b, BF),
                        v((16, 8, 1280), BF), v((16, 8, 1280), BF),
                        dma((5,)), dma((2, 4)), dma((2, 2, 4)), dma((2, 2, 4))]
        + [dma((2, 2, 4))] * 4 + [dma((2, 4))] * 2 + [dma((2, 2, 4))] * 2 + [dma((2, 2))] * 12 + [dma((16,))] * 2,
        compiler_params=pltpu.CompilerParams(collective_id=3, has_side_effects=True, vmem_limit_bytes=62 << 20),
        name="space_backward_and_reduce",
    )(backr, frames, refs, h1, qkv, rkv, o, full_s, full_t, dwt)


def finish_kernel(out, fg, rg, fin, out_o, fg_o, rg_o, *totals):
    out_o[...] = out[...]
    fg_o[...] = fg[...]
    rg_o[...] = rg[...].astype(F32)[:6].astype(BF)
    for h in range(2):
        for w in range(3):
            totals[4 * h + w][...] = fin[h, w].astype(F32)
        wide = fin[h, 3].astype(F32)
        totals[4 * h + 3][:, :640] = wide[:40]
        totals[4 * h + 3][:, 640:] = wide[40:]


def finish(out, fg, rg, fin):
    s = jax.ShapeDtypeStruct
    tall, flat = s((80, 640), F32), s((40, 1280), F32)
    return pl.pallas_call(
        finish_kernel,
        out_shape=(s((192, 1280), BF), s((192, 1280), BF), s((6, 1280), BF)) + (tall, tall, tall, flat) * 2,
        in_specs=[VM] * 4, out_specs=(VM,) * 11, name="write_outputs",
    )(out, fg, rg, fin)

def position_table(count, width):
    column = lax.broadcasted_iota(jnp.int32, (count, width), 1)
    frame = lax.broadcasted_iota(jnp.int32, (count, width), 0).astype(F32)
    rates = jnp.exp((column // 2).astype(F32) * (-2.0 * math.log(10000.0) / width))
    angles = frame * rates
    return jnp.where(column % 2 == 0, jnp.sin(angles), jnp.cos(angles))


def per_device(frames_in, ref_feats, out_grad, *weights):
    frames, grads = frames_in.reshape(192, 1280), out_grad.reshape(192, 1280)
    h1, qkv, rkv, o, h1r, ogr, refs, full_s, full_t = first(frames, ref_feats[0], grads, weights)
    backr, dwt = temporal(h1r, ogr, position_table(32, 1280), full_t)
    results = last(backr, frames, refs.reshape(128, 1280), h1, qkv, rkv, o, full_s, full_t, dwt)
    out, frames_grad, rg, *totals = finish(*results)
    return (out.reshape(frames_in.shape), frames_grad.reshape(frames_in.shape), rg[None], *totals)


def solution(mesh):
    rows, refs, weight = P("clip", "frame", None, None), P("clip", "frame", None), P("frame", None)
    return jax.shard_map(
        per_device, mesh=mesh, in_specs=(rows, refs, rows) + (weight,) * 8,
        out_specs=(rows, rows, refs) + (weight,) * 8, check_vma=False)
```

time: 255 us -> 192 us (0.75)
  Pallas kernels: 228 us -> 189 us
  local copies, waits for them, and re-layouts: 24.9 us -> 0 us
    pallas_call x4 -> x3, Pallas kernels: 201 us -> 160 us  [the longest x1 89.2 us: last(): pl.pallas_call(last_kernel, out_shape=(s((192, 1280), BF), s((192, 1280),...]
    unnamed x16 -> x0, local copies, waits for them, and re-layouts: 19.3 us -> none
where the time goes in v2:
time: 192 us; the launch traced here: 191 us
  Pallas kernels  189 us (98%)
    pallas_call x1, Pallas kernels, last(): pl.pallas_call(last_kernel, out_shape=(s((192, 1280), BF), s((192, 1280),...  89.2 us
    pallas_call x1, Pallas kernels, first(): pl.pallas_call(first_kernel, out_shape=(s((192, 1280), BF), s((3, 192, 64...  68 us
    pallas_call x1, Pallas kernels, temporal(): pl.pallas_call(time_kernel, out_shape=(s((256, 1920), BF), s((2, 2, 4, 4,...  28.6 us

profile of v2, /device:TPU:32, one launch (start us, length us, event | category | flops | bytes accessed | tf_op | source)
XLA Modules:
  0.0 190.8 jit_solution(565013971590603882)
XLA Ops:
  0.7 1.4 cosine_select_fusion.table
  2.0 68.0 %gather_and_space_forward.1 = (bf16[192,1280]{1,0:T(8,128)(2,1)}, bf16[3,192,640]{2,1,0:T(8,128)(2,1)}, bf16[2,96,640]{2,1,0:T(8,128)(2,1)}, bf16[192,640]{1,0:T...) custom-call(bf16[192,1280]{1,0:T(8,128)(2,1)} %bitcast.7, ...), custom_call_target="tpu_custom_call" | custom-call | tf_op jit(solution)/shard_map/gather_and_space_forward/pallas_call | solution.py:420
  70.1 28.6 %time_both.1 = (bf16[256,1920]{1,0:T(8,128)(2,1)}, bf16[2,2,4,4,80,640]{5,4,3,2,1,0:T(8,128)(2,1)}) custom-call(bf16[256,1280]{1,0:T(8,128)(2,1)} %get-tuple-element.37.h1r, bf16[256,1280]{1,0:T(8,128)(2,1)} %get-tuple-element.38.ogr, f32[32,1280]{1,0:T(8,128)} %cosine_select_fusion.table, bf16[16,4,80,640]{3,2,1,0:T(8,128)(2,1)} %get-tuple-element.39.full.full_t), custom_call_target="tpu_custom_call" | custom-call | tf_op jit(solution)/shard_map/time_both/pallas_call | solution.py:235
  98.6 89.2 %space_backward_and_reduce.1 = (bf16[192,1280]{1,0:T(8,128)(2,1)}, bf16[192,1280]{1,0:T(8,128)(2,1)}, bf16[8,1280]{1,0:T(8,128)(2,1)}, bf16[2,4,80,640]{3,2,1,0:T(8,128)(2,1)}) custom-call(bf16[256,1920]{1,0:T(8,128)(2,1)} %get-tuple-element.40.backr, bf16[192,1280]{1,0:T(8,128)(2,1)} %bitcast.8, bf16[128,1280]{1,0:T(8,128)(2,1)} %bitcast.10, ...), custom_call_target="tpu_custom_call" | custom-call | tf_op jit(solution)/shard_map/space_backward_and_reduce/pallas_call | solution.py:676
  187.9 3.0 %write_outputs.1 = (bf16[192,1280]{1,0:T(8,128)(2,1)}, bf16[192,1280]{1,0:T(8,128)(2,1)}, bf16[6,1280]{1,0:T(8,128)(2,1)}, f32[80,640]{1,0:T(8,128)}, f32[80,640...) custom-call(bf16[192,1280]{1,0:T(8,128)(2,1)} %get-tuple-element.48., ...), custom_call_target="tpu_custom_call" | custom-call | tf_op jit(solution)/shard_map/write_outputs/pallas_call | solution.py:707
  (4 shorter events, 0.0 us)

commit v3 on v2

v3 whole, which is shorter than its diff:
```python
import math

import jax
import jax.numpy as jnp
from jax import lax
from jax.experimental import pallas as pl
from jax.experimental.pallas import tpu as pltpu
from jax.sharding import PartitionSpec as P


MESH = pl.DeviceIdType.MESH
ANY = pl.BlockSpec(memory_space=pl.ANY)
VM = pl.BlockSpec(memory_space=pltpu.VMEM)


class Place:
    def __init__(self):
        clip, frame = lax.axis_index("clip"), lax.axis_index("frame")
        self.clip, self.frame = clip, frame
        self.x, self.zh = lax.rem(clip, 4), lax.div(clip, 4)
        self.y, self.zl, self.core = lax.div(frame, 4), lax.rem(lax.div(frame, 2), 2), lax.rem(frame, 2)
        self.parity = lax.rem(self.x, 2)
        self.sibling = (clip, frame + 1 - 2 * self.core)

    def along_y(self, step):
        return (self.clip, lax.rem(self.y + 4 + step, 4) * 4 + self.zl * 2 + self.core)

    def along_x(self, step):
        return (self.zh * 4 + lax.rem(self.x + 4 + step, 4), self.frame)

    def along_z(self, step):
        far = lax.rem(self.zh * 2 + self.zl + 8 + step, 8)
        return (lax.div(far, 2) * 4 + self.x, self.y * 4 + lax.rem(far, 2) * 2 + self.core)

    def along_zh(self, step):
        return (lax.rem(self.zh + 4 + step, 4) * 4 + self.x, self.frame)

    def peer(self, step):
        return (self.clip, lax.rem(self.frame + step, 16))


def greet(devices):
    barrier = pltpu.get_barrier_semaphore()
    for device in devices:
        pl.semaphore_signal(barrier, inc=1, device_id=device, device_id_type=MESH)
    pl.semaphore_wait(barrier, len(devices))


def remote(src, dst, send, recv, device):
    return pltpu.make_async_remote_copy(
        src_ref=src, dst_ref=dst, send_sem=send, recv_sem=recv, device_id=device, device_id_type=MESH)


def shard_of(y, zl, core):
    return lax.rem(y + 8, 4) * 4 + zl * 2 + core


BF, F32 = jnp.bfloat16, jnp.float32
EPSILON = 1e-05
SCALE = 160 ** -0.5


def dot(a, b, ca=1, cb=0):
    return lax.dot_general(a, b, (((ca,), (cb,)), ((), ())), preferred_element_type=F32)


def stats(wide):
    offset = wide - jnp.mean(wide, -1, keepdims=True)
    inverse = lax.rsqrt(jnp.mean(offset * offset, -1, keepdims=True) + EPSILON)
    return offset * inverse, inverse


def stats_back(centred, inverse, g):
    first = jnp.mean(g, -1, keepdims=True)
    second = jnp.mean(g * centred, -1, keepdims=True)
    return inverse * (g - first - centred * second)


def iota(shape, dim):
    return lax.broadcasted_iota(jnp.int32, shape, dim)


def one_hot(hit):
    return jnp.where(hit, 1.0, 0.0).astype(BF)


def frame_pack():
    r, c = iota((256, 192), 0), iota((256, 192), 1)
    d, j = lax.shift_right_logical(r, 4), lax.bitwise_and(r, 15)
    a = jnp.where(j >= 6, 1, 0)
    return one_hot((j < 12) & (c == 90 * a + 6 * d + j))


def frame_unpack():
    c, r = iota((192, 256), 0), iota((192, 256), 1)
    d, j = lax.shift_right_logical(r, 4), lax.bitwise_and(r, 15)
    a = jnp.where(j >= 6, 1, 0)
    return one_hot((j < 12) & (c == 90 * a + 6 * d + j))


def token_unpack():
    m, r = iota((192, 256), 0), iota((192, 256), 1)
    t, f, a = lax.shift_right_logical(m, 5), lax.bitwise_and(lax.shift_right_logical(m, 1), 15), lax.bitwise_and(m, 1)
    return one_hot(r == 16 * f + 6 * a + t)


def token_pack():
    m, r = iota((256, 192), 1), iota((256, 192), 0)
    t, f, a = lax.shift_right_logical(m, 5), lax.bitwise_and(lax.shift_right_logical(m, 1), 15), lax.bitwise_and(m, 1)
    return one_hot(r == 16 * f + 6 * a + t)


def ref_unpack(rows, cols, swap=False):
    m, r = (iota((rows, cols), 0), iota((rows, cols), 1)) if not swap else (iota((rows, cols), 1), iota((rows, cols), 0))
    d, j = lax.shift_right_logical(r, 3), lax.bitwise_and(r, 7)
    return one_hot((j < 6) & (m == 6 * d + j))


def head_masks():
    lane = iota((1, 640), 1)
    return [(lane >= 160 * h) & (lane < 160 * (h + 1)) for h in range(4)]


def stack_heads(rows, masks):
    return jnp.concatenate([rows * one_hot(m) for m in masks], 0)


def merge_heads(stacked, masks):
    n = stacked.shape[0] // 4
    total = jnp.where(masks[0], stacked[:n], 0.0)
    for h in range(1, 4):
        total = jnp.where(masks[h], stacked[h * n:(h + 1) * n], total)
    return total


def softmax(stacked, keys, same=None):
    powers = jnp.exp(dot(stacked, keys, 1, 1) * SCALE)
    if same is not None:
        powers = jnp.where(same, powers, 0.0)
    return powers / jnp.sum(powers, -1, keepdims=True)


def score_back(probs, grads, values):
    dp = dot(grads, values, 1, 1)
    return (probs * (dp - jnp.sum(probs * dp, -1, keepdims=True)) * SCALE).astype(BF)


def wide_output(slot):
    wide = slot.astype(F32)
    left = wide[:, :40].reshape(640, 640).astype(BF)
    right = wide[:, 40:].reshape(640, 640).astype(BF)
    return left, right


def pack_output(left, right):
    return jnp.concatenate([left.reshape(16, 40, 640), right.reshape(16, 40, 640)], 1)


def store_term(dw, w, term):
    parts = term.reshape(4, 2, 2, 80, 640).astype(BF)
    for core in range(2):
        for zl in range(2):
            dw[core, zl, w] = parts[:, zl, core]


def exchange_start(at, src, dst, send, recv):
    copies = []
    for i in range(1, 16):
        to = lax.rem(at.frame + i, 16)
        copy = remote(src.at[pl.ds(pl.multiple_of(16 * to, 16), 16)],
                      dst.at[pl.ds(pl.multiple_of(16 * at.frame, 16), 16)], send.at[i], recv.at[i], at.peer(i))
        copy.start()
        copies.append(copy)
    own = pl.ds(pl.multiple_of(16 * at.frame, 16), 16)
    dst[own, :] = src[own, :]
    return copies


def load(src, dst, sem):
    copy = pltpu.make_async_copy(src, dst, sem)
    copy.start()
    return copy


def add(*parts):
    total = parts[0].astype(F32)
    for part in parts[1:]:
        total = total + part.astype(F32)
    return total


def whole_kernel(frames, ref_in, og_in, table, w0, w1, w2, w3, w4, w5, w6, w7,
                 out_o, fg_o, rg, fin,
                 pack, ref8, full_s, full_t, refs, qkv, rkv, o_in, h1_in,
                 buf_b, h1r, buf_g, ogr, buf_o, o2r, buf, backr,
                 dws, dwt, r0, rx, rz, ry1, ry2, pm, rax1, rax2, rq, gr, rgr,
                 sib_s, sib_r, y_s, y_r, rel_s, rel_r, gz_s, gz_r, gx_s, gx_r, ref_s, ref_r, ex_s, ex_r, loc,
                 c_s, c_r, x_s, x_r, z_s, z_r, y1_s, y1_r, y2_s, y2_r,
                 a1_s, a1_r, a2_s, a2_r, q_s, q_r, qq_s, qq_r, g_s, g_r, gg_s, gg_r, e_s, e_r):
    at = Place()
    y, zl, core, p, me = at.y, at.zl, at.core, at.parity, at.frame
    x, zh, oz = at.x, at.zh, 1 - at.zl
    for i, w in enumerate((w0, w1, w2, None, w4, w5, w6)):
        if w is not None:
            pack[i] = w[...]
    for i, w in ((3, w3), (7, w7)):
        wide = w[...].astype(F32)
        pack[i] = jnp.concatenate([wide[:, :640], wide[:, 640:]], 0).astype(BF)
    small = ref_in[...].astype(F32)
    ref8[...] = jnp.concatenate([small, small[:2] * 0.0], 0).astype(BF)
    greet([at.peer(i) for i in range(1, 16)] + [at.along_x(1), at.along_x(-1), at.along_z(1), at.along_z(-1),
                                                at.along_zh(1), at.along_zh(-1)])
    sends = []

    def go(copy):
        copy.start()
        sends.append(copy)
        return copy

    steps = (1, -1)
    fulls = (full_s, full_t)
    keeps = []

    def gather_chain(h):
        full = fulls[h]
        rows = [shard_of(y + k, zl, core) for k in range(4)]
        over = [shard_of(y + k, 1 - zl, core) for k in range(4)]

        def pair(j):
            return pl.ds(2 * j, 2)

        def to_sibling(index, ref):
            go(remote(ref, ref, sib_s.at[h, index], sib_r.at[h, index], at.sibling))

        def z_send(k, src=None):
            for d in range(2):
                w = 2 * p + d
                dst = full.at[rows[k], w]
                go(remote(dst if src is None else src.at[4 * h + w], dst, gz_s.at[h, k, d], gz_r.at[h, k, d],
                          at.along_z(1 - 2 * d)))

        def z_wait(k):
            for d in range(2):
                ref = full.at[over[k], 2 * p + d]
                remote(ref, ref, gz_s.at[h, k, d], gz_r.at[h, k, d], at.along_z(1)).wait_recv()
                go(remote(ref, ref, gx_s.at[h, k, d], gx_r.at[h, k, d], at.along_x(1 - 2 * d)))
                to_sibling(7 + 2 * k + d, ref)

        def x_wait(k):
            for d in range(2):
                ref = full.at[over[k], 2 * (1 - p) + d]
                remote(ref, ref, gx_s.at[h, k, d], gx_r.at[h, k, d], at.along_x(1)).wait_recv()
                to_sibling(15 + 2 * k + d, ref)

        half = pl.ds(4 * h, 4)
        for j in range(2):
            for s, step in enumerate(steps):
                go(remote(pack.at[pl.ds(4 * h + 2 * j, 2)], full.at[me, pair(j)], y_s.at[h, s, j], y_r.at[h, s, j],
                          at.along_y(step)))
        z_send(0, pack)
        go(remote(pack.at[half], full.at[me], sib_s.at[h, 0], sib_r.at[h, 0], at.sibling))
        keeps.append(load(pack.at[half], full.at[me], loc.at[h]))
        yield
        for j in range(2):
            for s, step in enumerate(steps):
                ref = full.at[rows[(4 - step) % 4], pair(j)]
                remote(ref, ref, y_s.at[h, s, j], y_r.at[h, s, j], at.along_y(step)).wait_recv()
                if j == s:
                    go(remote(ref, ref, rel_s.at[h, j], rel_r.at[h, j], at.along_y(step)))
                to_sibling(1 + 2 * s + j, ref)
        z_send(1)
        z_send(3)
        yield
        z_wait(0)
        for j in range(2):
            ref = full.at[rows[2], pair(j)]
            remote(ref, ref, rel_s.at[h, j], rel_r.at[h, j], at.along_y(1)).wait_recv()
            to_sibling(5 + j, ref)
        z_send(2)
        yield
        z_wait(1)
        z_wait(3)
        x_wait(0)
        yield
        z_wait(2)
        x_wait(1)
        x_wait(3)
        yield
        x_wait(2)
        yield

        def sib_wait(index, ref):
            remote(ref, ref, sib_s.at[h, index], sib_r.at[h, index], at.sibling).wait_recv()

        other = [shard_of(y + k, zl, 1 - core) for k in range(4)]
        sib_wait(0, full.at[other[0]])
        for s, step in enumerate(steps):
            for j in range(2):
                sib_wait(1 + 2 * s + j, full.at[other[(4 - step) % 4], pair(j)])
        for j in range(2):
            sib_wait(5 + j, full.at[other[2], pair(j)])
        for k in range(4):
            for d in range(2):
                far = shard_of(y + k, 1 - zl, 1 - core)
                sib_wait(7 + 2 * k + d, full.at[far, 2 * p + d])
                sib_wait(15 + 2 * k + d, full.at[far, 2 * (1 - p) + d])

    def rem4(v):
        return lax.rem(v + 8, 4)

    cross = {}

    def send_cross(h, w):
        src = dws if h == 0 else dwt
        for a, zz in enumerate((oz, zl)):
            cross[h, a, w] = go(remote(src.at[1 - core, zz, w], r0.at[h, a, w], c_s.at[h, a, w], c_r.at[h, a, w],
                                       at.sibling))

    def chain(h):
        g = (dws if h == 0 else dwt).at[core]
        low, high = pl.ds(0, 48), pl.ds(48, 32)
        ys = [rem4(y + k) for k in range(4)]
        xc, zc = {}, {}

        def take(a, zz):
            for w in range(4):
                cross[h, a, w].wait_recv()
                g[zz, w] = add(g[zz, w], r0[h, a, w]).astype(BF)

        def x_take(k):
            for d in range(2):
                xc[k, d].wait_recv()
                w = 2 * p + d
                g[oz, w, ys[k]] = add(g[oz, w, ys[k]], rx[h, d, k]).astype(BF)
                zc[k, d] = go(remote(g.at[oz, w, ys[k]], rz.at[h, d, k], z_s.at[h, d, k], z_r.at[h, d, k],
                                     at.along_z(2 * d - 1)))

        def z_take(k):
            for d in range(2):
                zc[k, d].wait_recv()
                w = 2 * p + d
                g[zl, w, ys[k]] = add(g[zl, w, ys[k]], rz[h, d, k]).astype(BF)

        take(0, oz)
        for k in (2, 1, 3, 0):
            for d in range(2):
                xc[k, d] = go(remote(g.at[oz, 2 * (1 - p) + d, ys[k]], rx.at[h, d, k], x_s.at[h, d, k],
                                     x_r.at[h, d, k], at.along_x(2 * d - 1)))
        take(1, zl)
        yield
        x_take(2)
        yield
        x_take(1)
        yield
        z_take(2)
        y1 = [go(remote(g.at[zl, w, ys[2]], ry1.at[h, w], y1_s.at[h, w], y1_r.at[h, w],
                        at.along_y(-1 if w < 2 else 1))) for w in range(4)]
        yield
        x_take(3)
        x_take(0)
        yield
        z_take(1)
        z_take(3)
        yield
        for w in range(4):
            y1[w].wait_recv()
            on = ys[3 if w < 2 else 1]
            g[zl, w, on] = add(g[zl, w, on], ry1[h, w]).astype(BF)
        y2 = {}
        turn = [rem4(x + 2), rem4(x + 1), rem4(x + 3), x]
        for n, w in enumerate(turn):
            for s, step in enumerate((1, -1)):
                y2[s, n] = go(remote(g.at[zl, w, ys[step % 4]], ry2.at[s, h, n], y2_s.at[s, h, n],
                                     y2_r.at[s, h, n], at.along_y(step)))
        yield
        z_take(0)
        yield

        def y_take(n):
            y2[0, n].wait_recv()
            y2[1, n].wait_recv()
            pm[h, n] = add(g[zl, turn[n], y], ry2[0, h, n], ry2[1, h, n]).astype(BF)

        y_take(0)
        a1 = [go(remote(pm.at[h, 0, part], rax1.at[h, part], a1_s.at[h, s], a1_r.at[h, s], at.along_x(step)))
              for s, (step, part) in enumerate(((1, low), (-1, high)))]
        yield
        y_take(1)
        y_take(2)
        a2 = []
        for s, (step, part) in enumerate(((1, low), (-1, high))):
            a1[s].wait_recv()
            pm[h, 1 + s, part] = add(pm[h, 1 + s, part], rax1[h, part]).astype(BF)
            a2.append(go(remote(pm.at[h, 1 + s], rax2.at[s, h], a2_s.at[h, s], a2_r.at[h, s], at.along_x(step))))
        yield
        y_take(3)
        for copy in a2:
            copy.wait_recv()
        rq[h, zh] = add(pm[h, 3], rax2[0, h], rax2[1, h]).astype(BF)
        for s, step in enumerate((1, -1)):
            go(remote(rq.at[h, zh], rq.at[h, zh], q_s.at[h, s], q_r.at[h, s], at.along_zh(step)))
        yield
        for s, (step, part) in enumerate(((1, low), (-1, high))):
            ref = rq.at[h, rem4(zh - step)]
            remote(ref, ref, q_s.at[h, s], q_r.at[h, s], at.along_zh(step)).wait_recv()
            ref = rq.at[h, rem4(zh - step), part]
            go(remote(ref, ref, qq_s.at[h, s], qq_r.at[h, s], at.along_zh(step)))
        yield
        for s, (step, part) in enumerate(((1, low), (-1, high))):
            ref = rq.at[h, rem4(zh + 2), part]
            remote(ref, ref, qq_s.at[h, s], qq_r.at[h, s], at.along_zh(step)).wait_recv()
        fin[h, x] = add(rq[h, 0], rq[h, 1], rq[h, 2], rq[h, 3]).astype(BF)
        for s, step in enumerate((1, -1)):
            go(remote(fin.at[h, x], fin.at[h, x], g_s.at[h, s], g_r.at[h, s], at.along_x(step)))
        yield
        for s, (step, part) in enumerate(((1, low), (-1, high))):
            ref = fin.at[h, rem4(x - step)]
            remote(ref, ref, g_s.at[h, s], g_r.at[h, s], at.along_x(step)).wait_recv()
            ref = fin.at[h, rem4(x - step), part]
            go(remote(ref, ref, gg_s.at[h, s], gg_r.at[h, s], at.along_x(step)))
        yield
        for s, (step, part) in enumerate(((1, low), (-1, high))):
            ref = fin.at[h, rem4(x + 2), part]
            remote(ref, ref, gg_s.at[h, s], gg_r.at[h, s], at.along_x(step)).wait_recv()
        yield

    now, later = gather_chain(0), gather_chain(1)
    next(now)
    pack_rows = frame_pack()
    buf_g[...] = dot(pack_rows, og_in[...]).astype(BF)
    masks = head_masks()
    wide = frames[...].astype(F32)
    n1 = stats(wide)[0].astype(BF)
    next(now)
    for i in range(1, 16):
        go(remote(ref8, refs.at[me], ref_s.at[i], ref_r.at[i], at.peer(i)))
    refs[me] = ref8[...]
    next(now)
    next(later)
    next(now)
    next(now)
    next(now)
    for i in range(1, 16):
        ref = refs.at[lax.rem(me + 16 - i, 16)]
        remote(ref, ref, ref_s.at[i], ref_r.at[i], at.peer(i)).wait_recv()
    for _ in now:
        pass
    keeps[0].wait()
    ref = dot(ref_unpack(96, 128), refs[...].astype(F32).reshape(128, 1280).astype(BF)).astype(BF)
    q = dot(n1, full_s[:, 0].reshape(1280, 640)).astype(BF)
    w = full_s[:, 1].reshape(1280, 640)
    k, rk = dot(n1, w).astype(BF), dot(ref, w).astype(BF)
    next(later)
    w = full_s[:, 2].reshape(1280, 640)
    v, rv = dot(n1, w).astype(BF), dot(ref, w).astype(BF)
    for i, part in enumerate((q, k, v)):
        qkv[i] = part
    rkv[0] = rk
    rkv[1] = rv
    outs = []
    for a in range(2):
        rows = slice(96 * a, 96 * a + 96)
        keys = jnp.concatenate([k[rows], rk], 0)
        values = jnp.concatenate([v[rows], rv], 0)
        probs = softmax(stack_heads(q[rows], masks), keys).astype(BF)
        outs.append(merge_heads(dot(probs, values), masks))
        next(later)
    o = jnp.concatenate(outs, 0).astype(BF)
    o_in[...] = o
    left, right = wide_output(full_s[:, 3])
    h1 = (wide + jnp.concatenate([dot(o, left), dot(o, right)], 1)).astype(BF)
    h1_in[...] = h1
    buf_b[...] = dot(pack_rows, h1).astype(BF)
    copies = exchange_start(at, buf_b, h1r, ex_s.at[0], ex_r.at[0])
    to_owner = exchange_start(at, buf_g, ogr, ex_s.at[1], ex_r.at[1])
    for _ in later:
        pass
    for keep in keeps[1:]:
        keep.wait()
    for copy in copies:
        copy.wait_recv()
    unpack, t_pack = token_unpack(), token_pack()
    h1 = dot(unpack, h1r[...])
    centred, inverse = stats(h1)
    n2 = (centred + jnp.concatenate([table[...]] * 6, 0)).astype(BF)
    parts = []
    for i in range(3):
        parts.append(dot(n2, full_t[:, i].reshape(1280, 640)).astype(BF))
    q, k, v = parts
    r, c = iota((768, 192), 0), iota((768, 192), 1)
    r = jnp.where(r >= 384, r - 384, r)
    r = jnp.where(r >= 192, r - 192, r)
    same = lax.shift_right_logical(r, 5) == lax.shift_right_logical(c, 5)
    qs = stack_heads(q, masks)
    probs = softmax(qs, k, same)
    pb = probs.astype(BF)
    o2 = merge_heads(dot(pb, v), masks).astype(BF)
    buf_o[...] = dot(t_pack, o2).astype(BF)
    to_frame = exchange_start(at, buf_o, o2r, ex_s.at[2], ex_r.at[2])
    left, right = wide_output(full_t[:, 3])
    for copy in to_owner:
        copy.wait_recv()
    og = dot(unpack, ogr[...]).astype(BF)
    go2 = (dot(og[:, :640], left, 1, 1) + dot(og[:, 640:], right, 1, 1)).astype(BF)
    gs = stack_heads(go2, masks)
    eb = score_back(probs, gs, v)
    gq = merge_heads(dot(eb, k), masks).astype(BF)
    gk = dot(eb, qs, 0, 0).astype(BF)
    gv = dot(pb, gs, 0, 0).astype(BF)
    grads = (gq, gk, gv)
    gn = dot(gq, full_t[:, 0].reshape(1280, 640), 1, 1)
    for i in (1, 2):
        gn = gn + dot(grads[i], full_t[:, i].reshape(1280, 640), 1, 1)
    gh = (og.astype(F32) + stats_back(centred, inverse, gn)).astype(BF)
    buf[...] = dot(t_pack, gh).astype(BF)
    to_frame += exchange_start(at, buf, backr, ex_s.at[3], ex_r.at[3])
    for i in range(3):
        store_term(dwt, i, dot(n2, grads[i], 0, 0))
        send_cross(1, i)
    store_term(dwt, 3, pack_output(dot(o2, og[:, :640], 0, 0), dot(o2, og[:, 640:], 0, 0)))
    send_cross(1, 3)
    early = chain(1)
    for copy in to_frame:
        copy.wait_recv()
    f_unpack = frame_unpack()
    gh = dot(f_unpack, backr[...]).astype(BF)
    next(early)
    left, right = wide_output(full_s[:, 3])
    go_ = (dot(gh[:, :640], left, 1, 1) + dot(gh[:, 640:], right, 1, 1)).astype(BF)
    rk, rv = rkv[0], rkv[1]
    gq, gk, gv = [], [], []
    grk = grv = None
    for a in range(2):
        rows = slice(96 * a, 96 * a + 96)
        keys = jnp.concatenate([qkv[1, rows], rk], 0)
        values = jnp.concatenate([qkv[2, rows], rv], 0)
        qs = stack_heads(qkv[0, rows], masks)
        gs = stack_heads(go_[rows], masks)
        probs = softmax(qs, keys)
        eb = score_back(probs, gs, values)
        gq.append(merge_heads(dot(eb, keys), masks))
        gkeys = dot(eb, qs, 0, 0)
        gvalues = dot(probs.astype(BF), gs, 0, 0)
        gk.append(gkeys[:96])
        gv.append(gvalues[:96])
        grk = gkeys[96:] if grk is None else grk + gkeys[96:]
        grv = gvalues[96:] if grv is None else grv + gvalues[96:]
        next(early)
        next(early)
    gq, gk, gv = (jnp.concatenate(g, 0).astype(BF) for g in (gq, gk, gv))
    grk, grv = grk.astype(BF), grv.astype(BF)
    centred, inverse = stats(frames[...].astype(F32))
    n1 = centred.astype(BF)
    o = o_in[...]
    store_term(dws, 3, pack_output(dot(o, gh[:, :640], 0, 0), dot(o, gh[:, 640:], 0, 0)))
    send_cross(0, 3)
    store_term(dws, 0, dot(n1, gq, 0, 0))
    send_cross(0, 0)
    store_term(dws, 1, dot(n1, gk, 0, 0) + dot(ref, grk, 0, 0))
    send_cross(0, 1)
    store_term(dws, 2, dot(n1, gv, 0, 0) + dot(ref, grv, 0, 0))
    send_cross(0, 2)
    spread = ref_unpack(128, 96, True)
    gr[:, :, :640] = dot(spread, grk).reshape(16, 8, 640).astype(BF)
    gr[:, :, 640:] = dot(spread, grv).reshape(16, 8, 640).astype(BF)
    rgr[me] = gr[me]
    late = chain(0)
    next(late)
    next(early)
    for i in range(1, 16):
        to = lax.rem(me + i, 16)
        go(remote(gr.at[to], rgr.at[me], e_s.at[i], e_r.at[i], at.peer(i)))

    def finish_rows():
        gn = None
        for n, (i, g) in enumerate(((0, gq), (1, gk), (2, gv))):
            term = dot(g, full_s[:, n].reshape(1280, 640), 1, 1)
            gn = term if gn is None else gn + term
        fg_o[...] = (gh.astype(F32) + stats_back(centred, inverse, gn)).astype(BF)

    def finish_out():
        left, right = wide_output(full_t[:, 3])
        o2 = dot(f_unpack, o2r[...]).astype(BF)
        out_o[...] = (h1_in[...].astype(F32) + jnp.concatenate([dot(o2, left), dot(o2, right)], 1)).astype(BF)

    def finish_ref():
        for i in range(1, 16):
            got = rgr.at[lax.rem(me + 16 - i, 16)]
            remote(got, got, e_s.at[i], e_r.at[i], at.peer(i)).wait_recv()
        total = rgr[0].astype(F32)
        for i in range(1, 16):
            total = total + rgr[i].astype(F32)
        total = total.astype(BF)
        rg[...] = (dot(total[:, :640], full_s[:, 1].reshape(1280, 640), 1, 1)
                   + dot(total[:, 640:], full_s[:, 2].reshape(1280, 640), 1, 1)).astype(BF)

    work = {"A": finish_rows, "B": finish_out, "C": finish_ref}
    for step in "TTATSTSSBTSSSCSTSSTSTSTSSS":
        if step in work:
            work[step]()
        else:
            next(early if step == "T" else late)
    for copy in copies + to_owner + to_frame + sends:
        copy.wait_send()


def whole(frames, ref_in, og, table, weights):
    dma = pltpu.SemaphoreType.DMA
    s = jax.ShapeDtypeStruct
    v = pltpu.VMEM
    b = (80, 640)
    wide = v((256, 1280), BF)
    return pl.pallas_call(
        whole_kernel,
        out_shape=(s((192, 1280), BF), s((192, 1280), BF), s((8, 1280), BF), s((2, 4) + b, BF)),
        in_specs=[VM] * 12,
        out_specs=(VM,) * 4,
        scratch_shapes=[v((8,) + b, BF), v((8, 1280), BF), v((16, 4) + b, BF), v((16, 4) + b, BF),
                        v((16, 8, 1280), BF), v((3, 192, 640), BF), v((2, 96, 640), BF), v((192, 640), BF),
                        v((192, 1280), BF), wide, wide, wide, wide, v((256, 640), BF), v((256, 640), BF), wide, wide,
                        v((2, 2, 4, 4) + b, BF), v((2, 2, 4, 4) + b, BF), v((2, 2, 4, 4) + b, BF),
                        v((2, 2, 4) + b, BF), v((2, 2, 4) + b, BF), v((2, 4) + b, BF), v((2, 2, 4) + b, BF),
                        v((2, 4) + b, BF), v((2,) + b, BF), v((2, 2) + b, BF), v((2, 4) + b, BF),
                        v((16, 8, 1280), BF), v((16, 8, 1280), BF)]
        + [dma((2, 23))] * 2 + [dma((2, 2, 2))] * 2 + [dma((2, 2))] * 2 + [dma((2, 4, 2))] * 4 + [dma((16,))] * 2
        + [dma((4, 16))] * 2 + [dma((2,))]
        + [dma((2, 2, 4))] * 6 + [dma((2, 4))] * 2 + [dma((2, 2, 4))] * 2 + [dma((2, 2))] * 12 + [dma((16,))] * 2,
        compiler_params=pltpu.CompilerParams(collective_id=0, has_side_effects=True,
                                             vmem_limit_bytes=67043328),
        name="whole",
    )(frames, ref_in, og, table, *weights)


def finish_kernel(out, fg, rg, fin, out_o, fg_o, rg_o, *totals):
    out_o[...] = out[...]
    fg_o[...] = fg[...]
    rg_o[...] = rg[...].astype(F32)[:6].astype(BF)
    for h in range(2):
        for w in range(3):
            totals[4 * h + w][...] = fin[h, w].astype(F32)
        wide = fin[h, 3].astype(F32)
        totals[4 * h + 3][:, :640] = wide[:40]
        totals[4 * h + 3][:, 640:] = wide[40:]


def finish(out, fg, rg, fin):
    s = jax.ShapeDtypeStruct
    tall, flat = s((80, 640), F32), s((40, 1280), F32)
    return pl.pallas_call(
        finish_kernel,
        out_shape=(s((192, 1280), BF), s((192, 1280), BF), s((6, 1280), BF)) + (tall, tall, tall, flat) * 2,
        in_specs=[VM] * 4, out_specs=(VM,) * 11, name="write_outputs",
    )(out, fg, rg, fin)

def position_table(count, width):
    column = lax.broadcasted_iota(jnp.int32, (count, width), 1)
    frame = lax.broadcasted_iota(jnp.int32, (count, width), 0).astype(F32)
    rates = jnp.exp((column // 2).astype(F32) * (-2.0 * math.log(10000.0) / width))
    angles = frame * rates
    return jnp.where(column % 2 == 0, jnp.sin(angles), jnp.cos(angles))


def per_device(frames_in, ref_feats, out_grad, *weights):
    frames, grads = frames_in.reshape(192, 1280), out_grad.reshape(192, 1280)
    results = whole(frames, ref_feats[0], grads, position_table(32, 1280), weights)
    out, frames_grad, rg, *totals = finish(*results)
    return (out.reshape(frames_in.shape), frames_grad.reshape(frames_in.shape), rg[None], *totals)


def solution(mesh):
    rows, refs, weight = P("clip", "frame", None, None), P("clip", "frame", None), P("frame", None)
    return jax.shard_map(
        per_device, mesh=mesh, in_specs=(rows, refs, rows) + (weight,) * 8,
        out_specs=(rows, rows, refs) + (weight,) * 8, check_vma=False)
```

time: 192 us -> 170 us (0.89)
  Pallas kernels: 189 us -> 168 us
    pallas_call x3 -> x1, Pallas kernels: 186 us -> 165 us  [whole(): pl.pallas_call(whole_kernel, out_shape=(s((192, 1280), BF), s((192, 1280)...]
where the time goes in v3:
time: 170 us
  Pallas kernels  168 us (99%)
    pallas_call x1, Pallas kernels, whole(): pl.pallas_call(whole_kernel, out_shape=(s((192, 1280), BF), s((192, 1280)...  165 us

profile of v3, /device:TPU:32, one launch (start us, length us, event | category | flops | bytes accessed | tf_op | source)
XLA Modules:
  0.0 169.7 jit_solution(6920973003777413194)
XLA Ops:
  0.7 1.4 cosine_select_fusion.table
  2.0 164.6 %whole.1 = (bf16[192,1280]{1,0:T(8,128)(2,1)}, bf16[192,1280]{1,0:T(8,128)(2,1)}, bf16[8,1280]{1,0:T(8,128)(2,1)}, bf16[2,4,80,640]{3,2,1,0:T(8,128)(2,1)}) custom-call(bf16[192,1280]{1,0:T(8,128)(2,1)} %bitcast.6, bf16[6,1280]{1,0:T(8,128)(2,1)} %bitcast.8, bf16[192,1280]{1,0:T(8,128)(2,1)} %bitcast.7, f32[32,1280]{1,0:T(8,128)} %cosine_select_fusion.table, ...), custom_call_target="tpu_custom_call" | custom-call | tf_op jit(solution)/shard_map/whole/pallas_call | solution.py:613
  166.7 3.0 %write_outputs.1 = (bf16[192,1280]{1,0:T(8,128)(2,1)}, bf16[192,1280]{1,0:T(8,128)(2,1)}, bf16[6,1280]{1,0:T(8,128)(2,1)}, f32[80,640]{1,0:T(8,128)}, f32[80,640...) custom-call(bf16[192,1280]{1,0:T(8,128)(2,1)} %get-tuple-element.26., ...), custom_call_target="tpu_custom_call" | custom-call | tf_op jit(solution)/shard_map/write_outputs/pallas_call | solution.py:649
  (4 shorter events, 0.0 us)

commit v4 on v3

--- a/solution.py
+++ b/solution.py
@@ -189,10 +189,21 @@
     return total
 
 
-def whole_kernel(frames, ref_in, og_in, table, w0, w1, w2, w3, w4, w5, w6, w7,
+def position_table(count, width):
+    column = lax.broadcasted_iota(jnp.int32, (count, width), 1)
+    frame = lax.broadcasted_iota(jnp.int32, (count, width), 0).astype(F32)
+    rates = jnp.exp((column // 2).astype(F32) * (-2.0 * math.log(10000.0) / width))
+    angles = frame * rates
+    return jnp.where(column % 2 == 0, jnp.sin(angles), jnp.cos(angles))
+
+
+ORDER = "SSTTSSATSTSSBTSSCTSTSTTSSS"
+
+
+def whole_kernel(frames, ref_in, og_in, w0, w1, w2, w3, w4, w5, w6, w7,
                  out_o, fg_o, rg, fin,
                  pack, ref8, full_s, full_t, refs, qkv, rkv, o_in, h1_in,
-                 buf_b, h1r, buf_g, ogr, buf_o, o2r, buf, backr,
+                 table, buf_b, h1r, buf_g, ogr, buf_o, o2r, buf, backr,
                  dws, dwt, r0, rx, rz, ry1, ry2, pm, rax1, rax2, rq, gr, rgr,
                  sib_s, sib_r, y_s, y_r, rel_s, rel_r, gz_s, gz_r, gx_s, gx_r, ref_s, ref_r, ex_s, ex_r, loc,
                  c_s, c_r, x_s, x_r, z_s, z_r, y1_s, y1_r, y2_s, y2_r,
@@ -322,8 +333,8 @@
         ys = [rem4(y + k) for k in range(4)]
         xc, zc = {}, {}
 
-        def take(a, zz):
-            for w in range(4):
+        def take(a, zz, weights):
+            for w in weights:
                 cross[h, a, w].wait_recv()
                 g[zz, w] = add(g[zz, w], r0[h, a, w]).astype(BF)
 
@@ -341,12 +352,14 @@
                 w = 2 * p + d
                 g[zl, w, ys[k]] = add(g[zl, w, ys[k]], rz[h, d, k]).astype(BF)
 
-        take(0, oz)
+        take(0, oz, (0, 3))
+        yield
+        take(0, oz, (1, 2))
         for k in (2, 1, 3, 0):
             for d in range(2):
                 xc[k, d] = go(remote(g.at[oz, 2 * (1 - p) + d, ys[k]], rx.at[h, d, k], x_s.at[h, d, k],
                                      x_r.at[h, d, k], at.along_x(2 * d - 1)))
-        take(1, zl)
+        take(1, zl, (0, 3, 1, 2))
         yield
         x_take(2)
         yield
@@ -397,29 +410,36 @@
         for copy in a2:
             copy.wait_recv()
         rq[h, zh] = add(pm[h, 3], rax2[0, h], rax2[1, h]).astype(BF)
-        for s, step in enumerate((1, -1)):
-            go(remote(rq.at[h, zh], rq.at[h, zh], q_s.at[h, s], q_r.at[h, s], at.along_zh(step)))
-        yield
-        for s, (step, part) in enumerate(((1, low), (-1, high))):
-            ref = rq.at[h, rem4(zh - step)]
-            remote(ref, ref, q_s.at[h, s], q_r.at[h, s], at.along_zh(step)).wait_recv()
+        both = ((1, low, high), (-1, high, low))
+        for n in range(2):
+            for s, (step, *parts) in enumerate(both):
+                ref = rq.at[h, zh, parts[n]]
+                go(remote(ref, ref, q_s.at[h, s, n], q_r.at[h, s, n], at.along_zh(step)))
+        yield
+        for s, (step, part, _) in enumerate(both):
             ref = rq.at[h, rem4(zh - step), part]
+            remote(ref, ref, q_s.at[h, s, 0], q_r.at[h, s, 0], at.along_zh(step)).wait_recv()
             go(remote(ref, ref, qq_s.at[h, s], qq_r.at[h, s], at.along_zh(step)))
         yield
-        for s, (step, part) in enumerate(((1, low), (-1, high))):
+        for s, (step, part, rest) in enumerate(both):
+            ref = rq.at[h, rem4(zh - step), rest]
+            remote(ref, ref, q_s.at[h, s, 1], q_r.at[h, s, 1], at.along_zh(step)).wait_recv()
             ref = rq.at[h, rem4(zh + 2), part]
             remote(ref, ref, qq_s.at[h, s], qq_r.at[h, s], at.along_zh(step)).wait_recv()
         fin[h, x] = add(rq[h, 0], rq[h, 1], rq[h, 2], rq[h, 3]).astype(BF)
-        for s, step in enumerate((1, -1)):
-            go(remote(fin.at[h, x], fin.at[h, x], g_s.at[h, s], g_r.at[h, s], at.along_x(step)))
-        yield
-        for s, (step, part) in enumerate(((1, low), (-1, high))):
-            ref = fin.at[h, rem4(x - step)]
-            remote(ref, ref, g_s.at[h, s], g_r.at[h, s], at.along_x(step)).wait_recv()
+        for n in range(2):
+            for s, (step, *parts) in enumerate(both):
+                ref = fin.at[h, x, parts[n]]
+                go(remote(ref, ref, g_s.at[h, s, n], g_r.at[h, s, n], at.along_x(step)))
+        yield
+        for s, (step, part, _) in enumerate(both):
             ref = fin.at[h, rem4(x - step), part]
+            remote(ref, ref, g_s.at[h, s, 0], g_r.at[h, s, 0], at.along_x(step)).wait_recv()
             go(remote(ref, ref, gg_s.at[h, s], gg_r.at[h, s], at.along_x(step)))
         yield
-        for s, (step, part) in enumerate(((1, low), (-1, high))):
+        for s, (step, part, rest) in enumerate(both):
+            ref = fin.at[h, rem4(x - step), rest]
+            remote(ref, ref, g_s.at[h, s, 1], g_r.at[h, s, 1], at.along_x(step)).wait_recv()
             ref = fin.at[h, rem4(x + 2), part]
             remote(ref, ref, gg_s.at[h, s], gg_r.at[h, s], at.along_x(step)).wait_recv()
         yield
@@ -431,6 +451,7 @@
     masks = head_masks()
     wide = frames[...].astype(F32)
     n1 = stats(wide)[0].astype(BF)
+    table[...] = position_table(32, 1280)
     next(now)
     for i in range(1, 16):
         go(remote(ref8, refs.at[me], ref_s.at[i], ref_r.at[i], at.peer(i)))
@@ -520,6 +541,7 @@
     store_term(dwt, 3, pack_output(dot(o2, og[:, :640], 0, 0), dot(o2, og[:, 640:], 0, 0)))
     send_cross(1, 3)
     early = chain(1)
+    next(early)
     for copy in to_frame:
         copy.wait_recv()
     f_unpack = frame_unpack()
@@ -558,14 +580,15 @@
     send_cross(0, 0)
     store_term(dws, 1, dot(n1, gk, 0, 0) + dot(ref, grk, 0, 0))
     send_cross(0, 1)
+    late = chain(0)
     store_term(dws, 2, dot(n1, gv, 0, 0) + dot(ref, grv, 0, 0))
     send_cross(0, 2)
+    next(late)
+    next(late)
     spread = ref_unpack(128, 96, True)
     gr[:, :, :640] = dot(spread, grk).reshape(16, 8, 640).astype(BF)
     gr[:, :, 640:] = dot(spread, grv).reshape(16, 8, 640).astype(BF)
     rgr[me] = gr[me]
-    late = chain(0)
-    next(late)
     next(early)
     for i in range(1, 16):
         to = lax.rem(me + i, 16)
@@ -595,7 +618,7 @@
                    + dot(total[:, 640:], full_s[:, 2].reshape(1280, 640), 1, 1)).astype(BF)
 
     work = {"A": finish_rows, "B": finish_out, "C": finish_ref}
-    for step in "TTATSTSSBTSSSCSTSSTSTSTSSS":
+    for step in ORDER:
         if step in work:
             work[step]()
         else:
@@ -604,7 +627,7 @@
         copy.wait_send()
 
 
-def whole(frames, ref_in, og, table, weights):
+def whole(frames, ref_in, og, weights):
     dma = pltpu.SemaphoreType.DMA
     s = jax.ShapeDtypeStruct
     v = pltpu.VMEM
@@ -613,22 +636,23 @@
     return pl.pallas_call(
         whole_kernel,
         out_shape=(s((192, 1280), BF), s((192, 1280), BF), s((8, 1280), BF), s((2, 4) + b, BF)),
-        in_specs=[VM] * 12,
+        in_specs=[VM] * 11,
         out_specs=(VM,) * 4,
         scratch_shapes=[v((8,) + b, BF), v((8, 1280), BF), v((16, 4) + b, BF), v((16, 4) + b, BF),
                         v((16, 8, 1280), BF), v((3, 192, 640), BF), v((2, 96, 640), BF), v((192, 640), BF),
-                        v((192, 1280), BF), wide, wide, wide, wide, v((256, 640), BF), v((256, 640), BF), wide, wide,
+                        v((192, 1280), BF), v((32, 1280), F32), wide, wide, wide, wide, v((256, 640), BF), v((256, 640), BF), wide, wide,
                         v((2, 2, 4, 4) + b, BF), v((2, 2, 4, 4) + b, BF), v((2, 2, 4, 4) + b, BF),
                         v((2, 2, 4) + b, BF), v((2, 2, 4) + b, BF), v((2, 4) + b, BF), v((2, 2, 4) + b, BF),
                         v((2, 4) + b, BF), v((2,) + b, BF), v((2, 2) + b, BF), v((2, 4) + b, BF),
                         v((16, 8, 1280), BF), v((16, 8, 1280), BF)]
         + [dma((2, 23))] * 2 + [dma((2, 2, 2))] * 2 + [dma((2, 2))] * 2 + [dma((2, 4, 2))] * 4 + [dma((16,))] * 2
         + [dma((4, 16))] * 2 + [dma((2,))]
-        + [dma((2, 2, 4))] * 6 + [dma((2, 4))] * 2 + [dma((2, 2, 4))] * 2 + [dma((2, 2))] * 12 + [dma((16,))] * 2,
+        + [dma((2, 2, 4))] * 6 + [dma((2, 4))] * 2 + [dma((2, 2, 4))] * 2 + [dma((2, 2))] * 4 + [dma((2, 2, 2))] * 2
+        + [dma((2, 2))] * 2 + [dma((2, 2, 2))] * 2 + [dma((2, 2))] * 2 + [dma((16,))] * 2,
         compiler_params=pltpu.CompilerParams(collective_id=0, has_side_effects=True,
                                              vmem_limit_bytes=67043328),
         name="whole",
-    )(frames, ref_in, og, table, *weights)
+    )(frames, ref_in, og, *weights)
 
 
 def finish_kernel(out, fg, rg, fin, out_o, fg_o, rg_o, *totals):
@@ -652,17 +676,9 @@
         in_specs=[VM] * 4, out_specs=(VM,) * 11, name="write_outputs",
     )(out, fg, rg, fin)
 
-def position_table(count, width):
-    column = lax.broadcasted_iota(jnp.int32, (count, width), 1)
-    frame = lax.broadcasted_iota(jnp.int32, (count, width), 0).astype(F32)
-    rates = jnp.exp((column // 2).astype(F32) * (-2.0 * math.log(10000.0) / width))
-    angles = frame * rates
-    return jnp.where(column % 2 == 0, jnp.sin(angles), jnp.cos(angles))
-
-
 def per_device(frames_in, ref_feats, out_grad, *weights):
     frames, grads = frames_in.reshape(192, 1280), out_grad.reshape(192, 1280)
-    results = whole(frames, ref_feats[0], grads, position_table(32, 1280), weights)
+    results = whole(frames, ref_feats[0], grads, weights)
     out, frames_grad, rg, *totals = finish(*results)
     return (out.reshape(frames_in.shape), frames_grad.reshape(frames_in.shape), rg[None], *totals)
 

time: 170 us -> 163 us (0.959)
  Pallas kernels: 168 us -> 162 us
    pallas_call x1, Pallas kernels: 165 us -> 159 us  [whole(): pl.pallas_call(whole_kernel, out_shape=(s((192, 1280), BF), s((192, 1280)...]
where the time goes in v4:
time: 163 us
  Pallas kernels  162 us (99%)
    pallas_call x1, Pallas kernels, whole(): pl.pallas_call(whole_kernel, out_shape=(s((192, 1280), BF), s((192, 1280)...  159 us

profile of v4, /device:TPU:32, one launch (start us, length us, event | category | flops | bytes accessed | tf_op | source)
XLA Modules:
  0.0 163.1 jit_solution(7040007769706050151)
XLA Ops:
  0.6 159.5 %whole.1 = (bf16[192,1280]{1,0:T(8,128)(2,1)}, bf16[192,1280]{1,0:T(8,128)(2,1)}, bf16[8,1280]{1,0:T(8,128)(2,1)}, bf16[2,4,80,640]{3,2,1,0:T(8,128)(2,1)}) custom-call(bf16[192,1280]{1,0:T(8,128)(2,1)} %bitcast.6, bf16[6,1280]{1,0:T(8,128)(2,1)} %bitcast.8, bf16[192,1280]{1,0:T(8,128)(2,1)} %bitcast.7, bf16[80,640]{1,0:T(8,128)(2,1)} %w0.1, ...), custom_call_target="tpu_custom_call" | custom-call | tf_op jit(solution)/shard_map/whole/pallas_call | solution.py:636
  160.1 3.0 %write_outputs.1 = (bf16[192,1280]{1,0:T(8,128)(2,1)}, bf16[192,1280]{1,0:T(8,128)(2,1)}, bf16[6,1280]{1,0:T(8,128)(2,1)}, f32[80,640]{1,0:T(8,128)}, f32[80,640...) custom-call(bf16[192,1280]{1,0:T(8,128)(2,1)} %get-tuple-element.26., ...), custom_call_target="tpu_custom_call" | custom-call | tf_op jit(solution)/shard_map/write_outputs/pallas_call | solution.py:673

commit v5 on v4

--- a/solution.py
+++ b/solution.py
@@ -197,7 +197,7 @@
     return jnp.where(column % 2 == 0, jnp.sin(angles), jnp.cos(angles))
 
 
-ORDER = "SSTTSSATSTSSBTSSCTSTSTTSSS"
+ORDER = "ASSTTSBSTSTSSTSSCTSTSTTSSS"
 
 
 def whole_kernel(frames, ref_in, og_in, w0, w1, w2, w3, w4, w5, w6, w7,
@@ -453,10 +453,10 @@
     n1 = stats(wide)[0].astype(BF)
     table[...] = position_table(32, 1280)
     next(now)
+    next(now)
     for i in range(1, 16):
         go(remote(ref8, refs.at[me], ref_s.at[i], ref_r.at[i], at.peer(i)))
     refs[me] = ref8[...]
-    next(now)
     next(later)
     next(now)
     next(now)

time: 163 us -> 162 us (level)
    pallas_call x1, Pallas kernels: 159 us -> 158 us  [whole(): pl.pallas_call(whole_kernel, out_shape=(s((192, 1280), BF), s((192, 1280)...]
where the time goes in v5:
time: 162 us; the launch traced here: 161 us
  Pallas kernels  161 us (99%)
    pallas_call x1, Pallas kernels, whole(): pl.pallas_call(whole_kernel, out_shape=(s((192, 1280), BF), s((192, 1280)...  158 us

profile of v5, /device:TPU:32, one launch (start us, length us, event | category | flops | bytes accessed | tf_op | source)
XLA Modules:
  0.0 161.3 jit_solution(13725995057670251484)
XLA Ops:
  0.6 157.7 %whole.1 = (bf16[192,1280]{1,0:T(8,128)(2,1)}, bf16[192,1280]{1,0:T(8,128)(2,1)}, bf16[8,1280]{1,0:T(8,128)(2,1)}, bf16[2,4,80,640]{3,2,1,0:T(8,128)(2,1)}) custom-call(bf16[192,1280]{1,0:T(8,128)(2,1)} %bitcast.6, bf16[6,1280]{1,0:T(8,128)(2,1)} %bitcast.8, bf16[192,1280]{1,0:T(8,128)(2,1)} %bitcast.7, bf16[80,640]{1,0:T(8,128)(2,1)} %w0.1, ...), custom_call_target="tpu_custom_call" | custom-call | tf_op jit(solution)/shard_map/whole/pallas_call | solution.py:636
  158.3 3.0 %write_outputs.1 = (bf16[192,1280]{1,0:T(8,128)(2,1)}, bf16[192,1280]{1,0:T(8,128)(2,1)}, bf16[6,1280]{1,0:T(8,128)(2,1)}, f32[80,640]{1,0:T(8,128)}, f32[80,640...) custom-call(bf16[192,1280]{1,0:T(8,128)(2,1)} %get-tuple-element.26., ...), custom_call_target="tpu_custom_call" | custom-call | tf_op jit(solution)/shard_map/write_outputs/pallas_call | solution.py:673
